TPU v7x, 32 devices: a whole 2x2x4 slice. The times are simulated.
32 devices in a mesh: morton: 32 (over z, y, x, core).
Axes of the slice: x: 2, y: 2, z: 4, core: 2. Of those that a mesh axis runs over, the one named last changes fastest.
Arguments:
- offsets: float32 [3, 262144], P(None, 'morton'), may hold values from -0.5 to 0.5
- forces: float32 [3, 262144], P(None, 'morton'), may hold values from -6 to 6
- counts: int32 [2048], P('morton'), may hold values from 1 to 128
- uc2ue: float32 [456, 456], replicated, may hold values from -0.25 to 0.25
- m2m_ops: float32 [8, 456, 456], replicated, may hold values from -0.09375 to 0.09375
- compress: float32 [456, 64], replicated, may hold values from -0.25 to 0.25
- m2l_ops: bfloat16 [316, 64, 64], replicated, may hold values from -0.0546875 to 0.0546875
- root_ops: bfloat16 [7, 64, 64], replicated, may hold values from -0.375 to 0.375
Outputs:
- local_boxes: float32 [2336, 64], P('morton')
- local_roots: float32 [4, 64], replicated
Inputs may be any that keep to these rules, and one draw needn't show every extreme that they name: The live points of a leaf are its first counts slots; later slots belong to no point.
All inputs are finite; a program needn't handle non-finite values.
Results may differ from a plain program's by a relative error of at most 0.0031.
Values may be sent and summed in bfloat16 or wider, within the bound.
A program may use at most 192 MiB of HBM per device.

v0:
```python
import functools

import jax
import jax.numpy as jnp
import numpy as np
from jax import lax
from jax.experimental import pallas as pl
from jax.experimental.pallas import tpu as pltpu
from jax.sharding import PartitionSpec as P

SURF_ORDER = 6
NCOEF = 456
RANK = 64
P_CAP = 128
LEAF_DEV = 64


check_radius = 1.475
MESH = pl.DeviceIdType.MESH


def surface_points():
    tick_values = np.linspace(-1.0, 1.0, SURF_ORDER)
    chosen = []
    for along_x in range(SURF_ORDER):
        for along_y in range(SURF_ORDER):
            for along_z in range(SURF_ORDER):
                if (
                    min(along_x, along_y, along_z) == 0
                    or max(along_x, along_y, along_z) == SURF_ORDER - 1
                ):
                    chosen.append(
                        (tick_values[along_x], tick_values[along_y], tick_values[along_z])
                    )
    return check_radius * np.array(chosen).T


def two_parts(value):
    high = value.astype(jnp.bfloat16).astype(jnp.float32)
    return high, value - high


def product(value, high, low, contracted=0):
    rows = value.shape[0]
    parts = jnp.concatenate(two_parts(value), axis=0).astype(jnp.bfloat16)
    dims = (((1,), (contracted,)), ((), ()))
    both = lax.dot_general(parts, low, dims, preferred_element_type=jnp.float32)
    both += lax.dot_general(parts, high, dims, preferred_element_type=jnp.float32)
    return both[:rows] + both[rows:]


def halves(matrix):
    high, low = two_parts(matrix)
    return high.astype(jnp.bfloat16), low.astype(jnp.bfloat16)


def upward_kernel(counts_ref, offsets_ref, forces_ref, targets_ref, uc2ue_ref, compress_ref, m2m_hbm,
                  small_ref, block_ref, m2m, m2m_high, m2m_low, check, arrivals):
    f32, bf16 = jnp.float32, jnp.bfloat16
    points = NCOEF // 3
    octant = lax.axis_index("morton") % 8
    for o in range(8):
        pltpu.make_async_copy(m2m_hbm.at[o], m2m.at[o], arrivals.at[o]).start()
    check[...] = jnp.zeros_like(check)
    lane = lax.broadcasted_iota(jnp.int32, (8, 128), 1)
    lane_row = lax.broadcasted_iota(jnp.int32, (1, 128), 1)

    def one_leaf(leaf, carry):
        odd = (leaf >> 4 & 1) * 4 + (leaf >> 2 & 1) * 2 + (leaf & 1)
        parent = (leaf >> 5 & 1) * 4 + (leaf >> 3 & 1) * 2 + (leaf >> 1 & 1)
        here = lane == odd * 8 + parent
        slots = pl.ds(pl.multiple_of(leaf * P_CAP, P_CAP), P_CAP)
        live = lane_row < counts_ref[leaf]
        place = [jnp.broadcast_to(offsets_ref[s : s + 1, slots], (8, P_CAP)) for s in range(3)]
        force = [
            jnp.broadcast_to(jnp.where(live, forces_ref[s : s + 1, slots], 0.0), (8, P_CAP))
            for s in range(3)
        ]
        for first in range(0, points, 8):
            apart = [targets_ref[s * points + first : s * points + first + 8] - place[s] for s in range(3)]
            inverse = lax.rsqrt(apart[0] * apart[0] + apart[1] * apart[1] + apart[2] * apart[2])
            projected = apart[0] * force[0] + apart[1] * force[1] + apart[2] * force[2]
            scaled = projected * inverse * inverse
            for s in range(3):
                value = (force[s] + apart[s] * scaled) * inverse
                summed = jnp.sum(value, axis=1, keepdims=True)
                rows = slice(s * points + first, s * points + first + 8)
                check[rows] = jnp.where(here, summed, check[rows])
        return carry

    lax.fori_loop(0, LEAF_DEV, one_leaf, 0, unroll=2)

    potentials = jnp.transpose(check[...])[:LEAF_DEV, :NCOEF]
    leaf_density = product(potentials, *halves(uc2ue_ref[...]))
    mid_density = jnp.zeros((8, NCOEF), f32)
    for o in range(8):
        pltpu.make_async_copy(m2m_hbm.at[o], m2m.at[o], arrivals.at[o]).wait()
        high, low = halves(m2m[o])
        m2m_high[o] = high
        m2m_low[o] = low
        mid_density += product(leaf_density[8 * o : 8 * o + 8], high, low)
    own_density = jnp.zeros((8, NCOEF), f32)
    for o in range(8):
        child = jnp.broadcast_to(mid_density[o : o + 1], (8, NCOEF))
        own_density += product(child, m2m_high[o], m2m_low[o])
    lifted = product(own_density, m2m_high[octant], m2m_low[octant])
    stacked = jnp.concatenate([leaf_density, mid_density, own_density, lifted], axis=0)
    shrunk = product(stacked, *halves(compress_ref[...]), contracted=1)
    rounded = shrunk[:80].astype(bf16)
    row = lax.broadcasted_iota(jnp.int32, (80, 80), 0)
    col = lax.broadcasted_iota(jnp.int32, (80, 80), 1)
    odd = (row >> 4 & 1) * 4 + (row >> 2 & 1) * 2 + (row & 1)
    parent = (row >> 5 & 1) * 4 + (row >> 3 & 1) * 2 + (row >> 1 & 1)
    wanted = jnp.where(row < LEAF_DEV, odd * 8 + parent, row)
    ordered = jnp.dot(jnp.where(col == wanted, 1.0, 0.0).astype(bf16), rounded, preferred_element_type=f32)
    block_ref[...] = jnp.concatenate([ordered, ordered], axis=1).astype(bf16)
    small_ref[...] = jnp.concatenate([rounded.astype(f32)[72:80], shrunk[80:88]], axis=1)


def upward(offsets, forces, counts, uc2ue, m2m_ops, compress):
    vmem = pl.BlockSpec(memory_space=pltpu.VMEM)
    targets = np.repeat(surface_points().reshape(NCOEF, 1), P_CAP, axis=1)
    return pl.pallas_call(
        upward_kernel,
        out_shape=(
            jax.ShapeDtypeStruct((8, 128), jnp.float32),
            jax.ShapeDtypeStruct((80, 128), jnp.bfloat16),
        ),
        in_specs=[pl.BlockSpec(memory_space=pltpu.SMEM)] + [vmem] * 5 + [pl.BlockSpec(memory_space=pl.ANY)],
        out_specs=(vmem, vmem),
        scratch_shapes=[
            pltpu.VMEM(m2m_ops.shape, jnp.float32),
            pltpu.VMEM(m2m_ops.shape, jnp.bfloat16),
            pltpu.VMEM(m2m_ops.shape, jnp.bfloat16),
            pltpu.VMEM((512, 128), jnp.float32),
            pltpu.SemaphoreType.DMA((8,)),
        ],
    )(counts, offsets, forces, jnp.asarray(targets, dtype=jnp.float32), uc2ue, compress.T, m2m_ops)


def exchange_kernel(peers, small_ref, block_ref, stored_ref, root_ref, boxes_ref, roots_ref,
                    every, nearby, leaf_rows, mid_rows, operator_rows, padded, send_all, recv_all, send_near, recv_near):
    f32, bf16 = jnp.float32, jnp.bfloat16
    me = lax.axis_index("morton")
    columns_x, root_count = peers // 4, peers // 8
    column, y_bit, z_bit = me // 4, me // 2 % 2, me % 2
    own = me % 4
    barrier = pltpu.get_barrier_semaphore()

    def greet(k, carry):
        pl.semaphore_signal(barrier, inc=1, device_id=((me + k) % peers,), device_id_type=MESH)
        return carry

    lax.fori_loop(1, peers, greet, 0)

    def near_copy(number, arriving=False):
        dc, flip_y, flip_z = number // 4 - 1, number // 2 % 2, number % 2
        other = (y_bit + flip_y) % 2 * 2 + (z_bit + flip_z) % 2
        peer = (column + dc + columns_x) % columns_x * 4 + other
        return pltpu.make_async_remote_copy(
            src_ref=block_ref, dst_ref=nearby.at[1 - dc, other if arriving else own],
            send_sem=send_near.at[number], recv_sem=recv_near.at[number],
            device_id=(peer,), device_id_type=MESH)

    def small_copy(k, slot):
        return pltpu.make_async_remote_copy(
            src_ref=small_ref, dst_ref=every.at[slot], send_sem=send_all.at[k],
            recv_sem=recv_all.at[k], device_id=((me + k) % peers,), device_id_type=MESH)

    row = lax.broadcasted_iota(jnp.int32, (448, 128), 0)
    col = lax.broadcasted_iota(jnp.int32, (448, 128), 1)
    step_y = (row >> 6) - 3
    pair = (row >> 4) & 3
    half = col >> 6
    step_z = 2 * pair + half - 3 - (pair >> 1)
    usable = jnp.logical_not((pair == 2) & (half == 0))

    def chosen(side_bits, target, source, step, bit):
        target = (bit << side_bits) + target
        return (source - target == step) & (jnp.abs((source >> 1) - (target >> 1)) <= 1)

    leaf_select = (
        usable
        & chosen(2, (row >> 2) & 3, (((col >> 5) & 1) << 2) + ((col >> 2) & 3), step_y, y_bit)
        & chosen(2, row & 3, (((col >> 4) & 1) << 2) + (col & 3), step_z, z_bit)
    )
    leaf_select = jnp.where(leaf_select, 1.0, 0.0).astype(bf16)
    mid_base = (
        usable
        & ((row & 15) < 4)
        & ((col & 15) < 8)
        & chosen(1, (row >> 1) & 1, (((col >> 5) & 1) << 1) + ((col >> 1) & 1), step_y, y_bit)
        & chosen(1, row & 1, (((col >> 4) & 1) << 1) + (col & 1), step_z, z_bit)
    )
    mid_select = [
        jnp.where(mid_base & (((col >> 2) & 1) == lx), 1.0, 0.0).astype(bf16) for lx in range(2)
    ]
    on_diagonal = (
        lax.broadcasted_iota(jnp.int32, (128, 128), 0) >> 6
    ) == (lax.broadcasted_iota(jnp.int32, (128, 128), 1) >> 6)

    blank = jnp.zeros((28, 16, 128), bf16)
    leaf_rows[0] = blank
    leaf_rows[9] = blank
    mid_rows[0] = blank
    mid_rows[7] = blank

    pl.semaphore_wait(barrier, peers - 1)
    near_numbers = [number for number in range(12) if number != 4]
    for number in near_numbers:
        near_copy(number).start()

    def send_small(k, carry):
        small_copy(k, me).start()
        return carry

    lax.fori_loop(1, peers, send_small, 0)
    every[me] = small_ref[...]
    nearby[1, own] = block_ref[...]

    directions = stored_ref.shape[2]

    def turn(j, carry):
        pairs = jnp.concatenate([stored_ref[j], stored_ref[j + RANK // 2]], axis=0)
        turned = jnp.transpose(pairs).astype(f32)
        operator_rows[pl.ds(j, directions, stride=RANK), :] = turned[:, :RANK]
        operator_rows[pl.ds(j + RANK // 2, directions, stride=RANK), :] = turned[:, RANK:]
        return carry

    lax.fori_loop(0, RANK // 2, turn, 0, unroll=4)

    for number in near_numbers:
        near_copy(number, True).wait_recv()

    for c in range(3):
        inside = (column + c >= 1) & (column + c <= columns_x)
        diagonal = jnp.where(on_diagonal & inside, 1.0, 0.0).astype(bf16)

        def doubled(first):
            stack = nearby[c, :, first : first + 16, :].reshape(64, 128)
            return jnp.concatenate([stack, stack], axis=0) * diagonal

        for lx in range(4):
            plane = 4 * c + lx - 4
            if -2 <= plane <= 5:
                got = jnp.dot(leaf_select, doubled(16 * lx), preferred_element_type=f32)
                leaf_rows[plane + 3] = got.astype(bf16).reshape(28, 16, 128)
        sources = doubled(64)
        for lx in range(2):
            plane = 2 * c + lx - 2
            got = jnp.dot(mid_select[lx], sources, preferred_element_type=f32)
            mid_rows[plane + 3] = got.astype(bf16).reshape(28, 16, 128)

    bases = {-3: 0, -2: 49, 2: 218, 3: 267}
    first_direction = 0
    odd_target = (lax.broadcasted_iota(jnp.int32, (96, RANK), 0) >> 4) & 1
    total = jnp.zeros((96, RANK), f32)
    for u in range(7):
        part = jnp.zeros((96, RANK), f32)
        for v in range(7):

            def operand(a, b):
                halves = [
                    jnp.concatenate(
                        [
                            leaf_rows[u : u + 4, 4 * v + p].reshape(64, 128),
                            mid_rows[u : u + 2, 4 * v + p].reshape(32, 128),
                        ],
                        axis=0,
                    )
                    for p in (a, b)
                ]
                return jnp.concatenate(halves, axis=1)

            def operators(first):
                return operator_rows[first * RANK : (first + 4) * RANK].astype(bf16)

            if 2 <= u <= 4 and 2 <= v <= 4:
                part += jnp.dot(operand(0, 3), operators(first_direction), preferred_element_type=f32)
                first_direction += 4
            else:
                part += jnp.dot(operand(0, 1), operators(first_direction), preferred_element_type=f32)
                part += jnp.dot(operand(2, 3), operators(first_direction + 3), preferred_element_type=f32)
                first_direction += 7
        if u == 0:
            part = jnp.where(odd_target == 1, part, 0.0)
        if u == 6:
            part = jnp.where(odd_target == 0, part, 0.0)
        total += part
    boxes_ref[1:5] = total[64:68]
    boxes_ref[5:9] = total[80:84]
    boxes_ref[9:73] = total[:64]

    def small_arrived(k, carry):
        small_copy(k, (me - k + peers) % peers).wait_recv()
        return carry

    lax.fori_loop(1, peers, small_arrived, 0)

    own_total = jnp.zeros((8, RANK), f32)
    for u in (-3, -2, 2, 3):
        other = column + u
        good = (other >= 0) & (other < columns_x)
        if u == -3:
            good = good & (column % 2 == 1)
        if u == 3:
            good = good & (column % 2 == 0)
        wrapped = (other + 4 * columns_x) % columns_x
        part = jnp.zeros((8, RANK), f32)
        for sy in range(2):
            for sz in range(2):
                direction = bases[u] + (sy - y_bit + 3) * 7 + (sz - z_bit + 3)
                source = every[wrapped * 4 + sy * 2 + sz][:, :RANK].astype(bf16)
                rows = pl.ds(pl.multiple_of(direction * RANK, RANK), RANK)
                part += jnp.dot(source, operator_rows[rows].astype(bf16), preferred_element_type=f32)
        own_total += jnp.where(good, part, 0.0)
    boxes_ref[0:1] = own_total[:1]

    padded[...] = jnp.zeros_like(padded)
    for r in range(root_count):
        grouped = jnp.sum(every[8 * r : 8 * r + 8], axis=0)
        padded[root_count + r : root_count + r + 1] = grouped[:1]
    found = jnp.zeros((root_count, RANK), f32)
    for k in range(2 * root_count - 1):
        distance = k - (root_count - 1)
        if abs(distance) >= 2:
            start = root_count + distance
            source = padded[start : start + root_count, :][:, RANK:].astype(bf16)
            found += jnp.dot(source, root_ref[k], preferred_element_type=f32)
    roots_ref[...] = found

    for number in near_numbers:
        near_copy(number).wait_send()

    def small_sent(k, carry):
        small_copy(k, me).wait_send()
        return carry

    lax.fori_loop(1, peers, small_sent, 0)


def far_field(small, block, m2l_ops, root_ops):
    peers = lax.axis_size("morton")
    root_count = peers // 8
    vmem = pl.BlockSpec(memory_space=pltpu.VMEM)
    return pl.pallas_call(
        functools.partial(exchange_kernel, peers),
        out_shape=(
            jax.ShapeDtypeStruct((LEAF_DEV + 9, RANK), jnp.float32),
            jax.ShapeDtypeStruct((root_count, RANK), jnp.float32),
        ),
        in_specs=[vmem] * 4,
        out_specs=(vmem,) * 2,
        scratch_shapes=[
            pltpu.VMEM((peers, 8, 128), jnp.float32),
            pltpu.VMEM((3, 4, 80, 128), jnp.bfloat16),
            pltpu.VMEM((10, 28, 16, 128), jnp.bfloat16),
            pltpu.VMEM((8, 28, 16, 128), jnp.bfloat16),
            pltpu.VMEM(((m2l_ops.shape[0] // 8 + 2) * 8 * RANK, RANK), jnp.float32),
            pltpu.VMEM((3 * root_count, 128), jnp.float32),
            pltpu.SemaphoreType.DMA((peers,)),
            pltpu.SemaphoreType.DMA((peers,)),
            pltpu.SemaphoreType.DMA((12,)),
            pltpu.SemaphoreType.DMA((12,)),
        ],
        compiler_params=pltpu.CompilerParams(collective_id=0, has_side_effects=True),
    )(small, block, jnp.transpose(m2l_ops, (1, 2, 0)), root_ops)


def body(offsets, forces, counts, uc2ue, m2m_ops, compress, m2l_ops, root_ops):
    small, block = upward(offsets, forces, counts, uc2ue, m2m_ops, compress)
    local_boxes, local_roots = far_field(small, block, m2l_ops, root_ops)
    return (local_boxes, local_roots)


def solution(mesh):
    placed = (P(None, "morton"), P(None, "morton"), P("morton"), P(), P(), P(), P(), P())
    return jax.shard_map(
        body, mesh=mesh, in_specs=placed, out_specs=(P("morton", None), P()), check_vma=False
    )
```

profile of v0, /device:TPU:0, one launch (start us, length us, event | category | flops | bytes accessed | tf_op | source)
XLA Modules:
  0.0 39.2 jit_solution(10627726389382904960)
XLA Ops:
  0.6 13.4 %shard_map.104 = (f32[8,128]{1,0:T(8,128)}, bf16[80,128]{1,0:T(8,128)(2,1)}) custom-call(s32[64]{0:T(128)} %counts_ref.1, f32[3,8192]{1,0:T(4,128)} %offsets_ref.1, f32[3,8192]{1,0:T(4,128)} %forces_ref.1, f32[456,128]{1,0:T(8,128)} %constant.2.clone.targets_ref, f32[456,456]{1,0:T(8,128)} %uc2ue_ref.1, f32[64,456]{1,0:T(8,128)} %bitcast.3, ...), custom_call_target="tpu_custom_call" | custom-call | tf_op jit(solution)/shard_map/pallas_call | solution.py:123
  14.0 22.4 %shard_map.105 = (f32[73,64]{1,0:T(8,128)}, f32[4,64]{1,0:T(4,128)}) custom-call(f32[8,128]{1,0:T(8,128)} %get-tuple-element.4.small_ref, bf16[80,128]{1,0:T(8,128)(2,1)} %get-tuple-element.5.block_ref, bf16[64,64,316]{2,1,0:T(8,128)(2,1)} %bitcast.2, bf16[7,64,64]{2,1,0:T(8,128)(2,1)} %root_ref.1), custom_call_target="tpu_custom_call" | custom-call | tf_op jit(solution)/shard_map/pallas_call | solution.py:346
  36.5 1.5 %copy.11 = f32[73,64]{0,1:T(8,128)} copy(f32[73,64]{1,0:T(8,128)} %get-tuple-element.6) | data formatting | bytes 37376 | tf_op jit(solution)/shard_map/pallas_call | solution.py:346
  37.9 1.3 %copy.13 = f32[4,64]{1,0:T(4,128)} copy(f32[4,64]{1,0:T(4,128)} %get-tuple-element.11) | data formatting | bytes 2048
where the time goes:
time: 39.4 us; the launch traced here: 39.2 us
  Pallas kernels  35.8 us (91%)
  local copies, waits for them, and re-layouts  2.74 us (7%)
  between operations  0.65 us (2%)
    pallas_call x1, Pallas kernels, far_field(): pl.pallas_call(functools.partial(exchange_kernel, peers), out_shape=(jax....  22.4 us
    pallas_call x1, Pallas kernels, upward(): pl.pallas_call(upward_kernel, out_shape=(jax.ShapeDtypeStruct((8, 128), j...  13.4 us
    pallas_call x1, local copies, waits for them, and re-layouts, far_field(): pl.pallas_call(functools.partial(exchange_kernel, peers), out_shape=(jax....  1.48 us
    unnamed x1, local copies, waits for them, and re-layouts  1.26 us

commit v1 on v0

--- a/solution.py
+++ b/solution.py
@@ -13,6 +13,8 @@
 RANK = 64
 P_CAP = 128
 LEAF_DEV = 64
+HALF = RANK // 2
+PITCH = HALF + 8
 
 
 check_radius = 1.475
@@ -167,13 +169,12 @@
             src_ref=small_ref, dst_ref=every.at[slot], send_sem=send_all.at[k],
             recv_sem=recv_all.at[k], device_id=((me + k) % peers,), device_id_type=MESH)
 
-    row = lax.broadcasted_iota(jnp.int32, (448, 128), 0)
-    col = lax.broadcasted_iota(jnp.int32, (448, 128), 1)
-    step_y = (row >> 6) - 3
-    pair = (row >> 4) & 3
-    half = col >> 6
-    step_z = 2 * pair + half - 3 - (pair >> 1)
-    usable = jnp.logical_not((pair == 2) & (half == 0))
+    row = lax.broadcasted_iota(jnp.int32, (224, 256), 0)
+    col = lax.broadcasted_iota(jnp.int32, (224, 256), 1)
+    step_y = (row >> 5) - 3
+    slot = ((row >> 4) & 1) * 4 + (col >> 6)
+    step_z = jnp.where(slot < 4, slot - 3 + 3 * (slot >> 1), slot - 5)
+    usable = slot < 7
 
     def chosen(side_bits, target, source, step, bit):
         target = (bit << side_bits) + target
@@ -195,11 +196,11 @@
     mid_select = [
         jnp.where(mid_base & (((col >> 2) & 1) == lx), 1.0, 0.0).astype(bf16) for lx in range(2)
     ]
-    on_diagonal = (
-        lax.broadcasted_iota(jnp.int32, (128, 128), 0) >> 6
-    ) == (lax.broadcasted_iota(jnp.int32, (128, 128), 1) >> 6)
-
-    blank = jnp.zeros((28, 16, 128), bf16)
+    on_diagonal = (lax.broadcasted_iota(jnp.int32, (256, 256), 0) >> 6) == (
+        (lax.broadcasted_iota(jnp.int32, (256, 256), 1) >> 5) & 3
+    )
+
+    blank = jnp.zeros((14, 16, 256), bf16)
     leaf_rows[0] = blank
     leaf_rows[9] = blank
     mid_rows[0] = blank
@@ -221,13 +222,11 @@
     directions = stored_ref.shape[2]
 
     def turn(j, carry):
-        pairs = jnp.concatenate([stored_ref[j], stored_ref[j + RANK // 2]], axis=0)
-        turned = jnp.transpose(pairs).astype(f32)
-        operator_rows[pl.ds(j, directions, stride=RANK), :] = turned[:, :RANK]
-        operator_rows[pl.ds(j + RANK // 2, directions, stride=RANK), :] = turned[:, RANK:]
-        return carry
-
-    lax.fori_loop(0, RANK // 2, turn, 0, unroll=4)
+        pairs = jnp.concatenate([stored_ref[j], stored_ref[j + HALF]], axis=0)
+        operator_rows[pl.ds(j, directions, stride=PITCH), :] = jnp.transpose(pairs).astype(f32)
+        return carry
+
+    lax.fori_loop(0, HALF, turn, 0, unroll=4)
 
     for number in near_numbers:
         near_copy(number, True).wait_recv()
@@ -236,57 +235,58 @@
         inside = (column + c >= 1) & (column + c <= columns_x)
         diagonal = jnp.where(on_diagonal & inside, 1.0, 0.0).astype(bf16)
 
-        def doubled(first):
+        def spread(first):
             stack = nearby[c, :, first : first + 16, :].reshape(64, 128)
-            return jnp.concatenate([stack, stack], axis=0) * diagonal
+            low, high = stack[:, :HALF], stack[:, HALF:RANK]
+            wide = jnp.concatenate([low] * 4 + [high] * 4, axis=1)
+            return jnp.concatenate([wide] * 4, axis=0) * diagonal
 
         for lx in range(4):
             plane = 4 * c + lx - 4
             if -2 <= plane <= 5:
-                got = jnp.dot(leaf_select, doubled(16 * lx), preferred_element_type=f32)
-                leaf_rows[plane + 3] = got.astype(bf16).reshape(28, 16, 128)
-        sources = doubled(64)
+                got = jnp.dot(leaf_select, spread(16 * lx), preferred_element_type=f32)
+                leaf_rows[plane + 3] = got.astype(bf16).reshape(14, 16, 256)
+        sources = spread(64)
         for lx in range(2):
             plane = 2 * c + lx - 2
             got = jnp.dot(mid_select[lx], sources, preferred_element_type=f32)
-            mid_rows[plane + 3] = got.astype(bf16).reshape(28, 16, 128)
+            mid_rows[plane + 3] = got.astype(bf16).reshape(14, 16, 256)
 
     bases = {-3: 0, -2: 49, 2: 218, 3: 267}
     first_direction = 0
-    odd_target = (lax.broadcasted_iota(jnp.int32, (96, RANK), 0) >> 4) & 1
-    total = jnp.zeros((96, RANK), f32)
+    odd_target = (lax.broadcasted_iota(jnp.int32, (192, 128), 0) >> 4) & 1
+    total = jnp.zeros((192, 128), f32)
     for u in range(7):
-        part = jnp.zeros((96, RANK), f32)
+        part = jnp.zeros((192, 128), f32)
         for v in range(7):
 
-            def operand(a, b):
-                halves = [
-                    jnp.concatenate(
-                        [
-                            leaf_rows[u : u + 4, 4 * v + p].reshape(64, 128),
-                            mid_rows[u : u + 2, 4 * v + p].reshape(32, 128),
-                        ],
-                        axis=0,
-                    )
-                    for p in (a, b)
-                ]
-                return jnp.concatenate(halves, axis=1)
-
-            def operators(first):
-                return operator_rows[first * RANK : (first + 4) * RANK].astype(bf16)
+            def operand(quads):
+                rows = []
+                for lanes in (slice(0, 128), slice(128, 256)):
+                    for ref, count in ((leaf_rows, 4), (mid_rows, 2)):
+                        pieces = [
+                            ref[u : u + count, 2 * v + quad, :, lanes].reshape(16 * count, 128)
+                            for quad in quads
+                        ]
+                        rows.append(jnp.concatenate(pieces, axis=1))
+                return jnp.concatenate(rows, axis=0)
+
+            def operators(steps):
+                rows = [operator_rows[(first_direction + k) * PITCH : (first_direction + k) * PITCH + HALF] for k in steps]
+                return jnp.concatenate(rows, axis=0).astype(bf16)
 
             if 2 <= u <= 4 and 2 <= v <= 4:
-                part += jnp.dot(operand(0, 3), operators(first_direction), preferred_element_type=f32)
+                part += jnp.dot(operand((0,)), operators((0, 1, 2, 3)), preferred_element_type=f32)
                 first_direction += 4
             else:
-                part += jnp.dot(operand(0, 1), operators(first_direction), preferred_element_type=f32)
-                part += jnp.dot(operand(2, 3), operators(first_direction + 3), preferred_element_type=f32)
+                part += jnp.dot(operand((0, 1)), operators((0, 1, 5, 6, 2, 3, 4, 4)), preferred_element_type=f32)
                 first_direction += 7
         if u == 0:
             part = jnp.where(odd_target == 1, part, 0.0)
         if u == 6:
             part = jnp.where(odd_target == 0, part, 0.0)
         total += part
+    total = total[:96, :RANK] + total[96:, RANK:]
     boxes_ref[1:5] = total[64:68]
     boxes_ref[5:9] = total[80:84]
     boxes_ref[9:73] = total[:64]
@@ -310,9 +310,11 @@
         for sy in range(2):
             for sz in range(2):
                 direction = bases[u] + (sy - y_bit + 3) * 7 + (sz - z_bit + 3)
-                source = every[wrapped * 4 + sy * 2 + sz][:, :RANK].astype(bf16)
-                rows = pl.ds(pl.multiple_of(direction * RANK, RANK), RANK)
-                part += jnp.dot(source, operator_rows[rows].astype(bf16), preferred_element_type=f32)
+                source = every[wrapped * 4 + sy * 2 + sz].astype(bf16)
+                rows = pl.ds(pl.multiple_of(direction * PITCH, 8), HALF)
+                operator = operator_rows[rows].astype(bf16)
+                part += jnp.dot(source[:, :HALF], operator[:, :RANK], preferred_element_type=f32)
+                part += jnp.dot(source[:, HALF:RANK], operator[:, RANK:], preferred_element_type=f32)
         own_total += jnp.where(good, part, 0.0)
     boxes_ref[0:1] = own_total[:1]
 
@@ -354,9 +356,9 @@
         scratch_shapes=[
             pltpu.VMEM((peers, 8, 128), jnp.float32),
             pltpu.VMEM((3, 4, 80, 128), jnp.bfloat16),
-            pltpu.VMEM((10, 28, 16, 128), jnp.bfloat16),
-            pltpu.VMEM((8, 28, 16, 128), jnp.bfloat16),
-            pltpu.VMEM(((m2l_ops.shape[0] // 8 + 2) * 8 * RANK, RANK), jnp.float32),
+            pltpu.VMEM((10, 14, 16, 256), jnp.bfloat16),
+            pltpu.VMEM((8, 14, 16, 256), jnp.bfloat16),
+            pltpu.VMEM((m2l_ops.shape[0] * PITCH, 2 * RANK), jnp.float32),
             pltpu.VMEM((3 * root_count, 128), jnp.float32),
             pltpu.SemaphoreType.DMA((peers,)),
             pltpu.SemaphoreType.DMA((peers,)),

time: 39.4 us -> 36.1 us (0.916)
  Pallas kernels: 35.8 us -> 32.5 us
    pallas_call x1, Pallas kernels: 22.4 us -> 19.1 us  [far_field(): pl.pallas_call(functools.partial(exchange_kernel, peers), out_shape=(jax....]
where the time goes in v1:
time: 36.1 us; the launch traced here: 35.9 us
  Pallas kernels  32.5 us (90%)
  local copies, waits for them, and re-layouts  2.74 us (8%)
  between operations  0.65 us (2%)
    pallas_call x1, Pallas kernels, far_field(): pl.pallas_call(functools.partial(exchange_kernel, peers), out_shape=(jax....  19.1 us
    pallas_call x1, Pallas kernels, upward(): pl.pallas_call(upward_kernel, out_shape=(jax.ShapeDtypeStruct((8, 128), j...  13.4 us
    pallas_call x1, local copies, waits for them, and re-layouts, far_field(): pl.pallas_call(functools.partial(exchange_kernel, peers), out_shape=(jax....  1.48 us
    unnamed x1, local copies, waits for them, and re-layouts  1.26 us

profile of v1, /device:TPU:0, one launch (start us, length us, event | category | flops | bytes accessed | tf_op | source)
XLA Modules:
  0.0 35.9 jit_solution(13440714363750748297)
XLA Ops:
  0.6 13.4 %shard_map.104 = (f32[8,128]{1,0:T(8,128)}, bf16[80,128]{1,0:T(8,128)(2,1)}) custom-call(s32[64]{0:T(128)} %counts_ref.1, f32[3,8192]{1,0:T(4,128)} %offsets_ref.1, f32[3,8192]{1,0:T(4,128)} %forces_ref.1, f32[456,128]{1,0:T(8,128)} %constant.2.clone.targets_ref, f32[456,456]{1,0:T(8,128)} %uc2ue_ref.1, f32[64,456]{1,0:T(8,128)} %bitcast.3, ...), custom_call_target="tpu_custom_call" | custom-call | tf_op jit(solution)/shard_map/pallas_call | solution.py:125
  14.0 19.1 %shard_map.105 = (f32[73,64]{1,0:T(8,128)}, f32[4,64]{1,0:T(4,128)}) custom-call(f32[8,128]{1,0:T(8,128)} %get-tuple-element.4.small_ref, bf16[80,128]{1,0:T(8,128)(2,1)} %get-tuple-element.5.block_ref, bf16[64,64,316]{2,1,0:T(8,128)(2,1)} %bitcast.2, bf16[7,64,64]{2,1,0:T(8,128)(2,1)} %root_ref.1), custom_call_target="tpu_custom_call" | custom-call | tf_op jit(solution)/shard_map/pallas_call | solution.py:348
  33.1 1.5 %copy.11 = f32[73,64]{0,1:T(8,128)} copy(f32[73,64]{1,0:T(8,128)} %get-tuple-element.6) | data formatting | bytes 37376 | tf_op jit(solution)/shard_map/pallas_call | solution.py:348
  34.6 1.3 %copy.13 = f32[4,64]{1,0:T(4,128)} copy(f32[4,64]{1,0:T(4,128)} %get-tuple-element.11) | data formatting | bytes 2048

commit v2 on v1

v2 whole, which is shorter than its diff:
```python
import functools

import jax
import jax.numpy as jnp
import numpy as np
from jax import lax
from jax.experimental import pallas as pl
from jax.experimental.pallas import tpu as pltpu
from jax.sharding import PartitionSpec as P

SURF_ORDER = 6
NCOEF = 456
RANK = 64
P_CAP = 128
LEAF_DEV = 64
HALF = RANK // 2
PITCH = HALF + 8
FIRST_ROOT = (LEAF_DEV + 9 + 7) // 8 * 8


check_radius = 1.475
MESH = pl.DeviceIdType.MESH


def surface_points():
    tick_values = np.linspace(-1.0, 1.0, SURF_ORDER)
    chosen = []
    for along_x in range(SURF_ORDER):
        for along_y in range(SURF_ORDER):
            for along_z in range(SURF_ORDER):
                if (
                    min(along_x, along_y, along_z) == 0
                    or max(along_x, along_y, along_z) == SURF_ORDER - 1
                ):
                    chosen.append(
                        (tick_values[along_x], tick_values[along_y], tick_values[along_z])
                    )
    return check_radius * np.array(chosen).T


def two_parts(value):
    high = value.astype(jnp.bfloat16).astype(jnp.float32)
    return high, value - high


def product(value, high, low, contracted=0):
    rows = value.shape[0]
    parts = jnp.concatenate(two_parts(value), axis=0).astype(jnp.bfloat16)
    dims = (((1,), (contracted,)), ((), ()))
    both = lax.dot_general(parts, low, dims, preferred_element_type=jnp.float32)
    both += lax.dot_general(parts, high, dims, preferred_element_type=jnp.float32)
    return both[:rows] + both[rows:]


def halves(matrix):
    high, low = two_parts(matrix)
    return high.astype(jnp.bfloat16), low.astype(jnp.bfloat16)


def solver_kernel(peers, counts_ref, offsets_hbm, forces_hbm, targets_hbm, uc2ue_hbm, compress_hbm, m2m_hbm, stored_hbm, root_hbm,
                  packed_ref,
                  offsets_ref, forces_ref, targets_ref, uc2ue_ref, compress_ref, m2m, m2m_high, m2m_low, stored_ref, root_ref, check,
                  small_ref, block_ref, every, nearby, leaf_rows, mid_rows, operator_rows, padded,
                  loads, arrivals, send_all, recv_all, send_near, recv_near):
    f32, bf16 = jnp.float32, jnp.bfloat16
    points = NCOEF // 3
    me = lax.axis_index("morton")
    columns_x, root_count = peers // 4, peers // 8
    column, y_bit, z_bit = me // 4, me // 2 % 2, me % 2
    own, octant = me % 4, me % 8

    wholes = (
        (offsets_hbm, offsets_ref),
        (forces_hbm, forces_ref),
        (targets_hbm, targets_ref),
        (uc2ue_hbm, uc2ue_ref),
        (compress_hbm, compress_ref),
        (stored_hbm, stored_ref),
        (root_hbm, root_ref),
    )

    def load(number):
        return pltpu.make_async_copy(*wholes[number], loads.at[number])

    for number in range(5):
        load(number).start()
    for o in range(8):
        pltpu.make_async_copy(m2m_hbm.at[o], m2m.at[o], arrivals.at[o]).start()
    for number in range(5, 7):
        load(number).start()

    barrier = pltpu.get_barrier_semaphore()

    def greet(k, carry):
        pl.semaphore_signal(barrier, inc=1, device_id=((me + k) % peers,), device_id_type=MESH)
        return carry

    lax.fori_loop(1, peers, greet, 0)

    parts = {-1: (0, 32), 0: (0, 48), 1: (16, 48)}

    def near_copy(number, arriving=False):
        dc, flip_y, flip_z = number // 4 - 1, number // 2 % 2, number % 2
        other = (y_bit + flip_y) % 2 * 2 + (z_bit + flip_z) % 2
        peer = (column + dc + columns_x) % columns_x * 4 + other
        first, last = parts[dc]
        return pltpu.make_async_remote_copy(
            src_ref=block_ref.at[first:last],
            dst_ref=nearby.at[1 - dc, other if arriving else own, first:last],
            send_sem=send_near.at[number], recv_sem=recv_near.at[number],
            device_id=(peer,), device_id_type=MESH)

    def small_copy(k, slot):
        return pltpu.make_async_remote_copy(
            src_ref=small_ref, dst_ref=every.at[pl.ds(slot, 1)], send_sem=send_all.at[k],
            recv_sem=recv_all.at[k], device_id=((me + k) % peers,), device_id_type=MESH)

    for number in range(3):
        load(number).wait()
    check[...] = jnp.zeros_like(check)
    lane = lax.broadcasted_iota(jnp.int32, (8, 128), 1)
    lane_row = lax.broadcasted_iota(jnp.int32, (1, 128), 1)

    def one_leaf(leaf, carry):
        odd = (leaf >> 4 & 1) * 4 + (leaf >> 2 & 1) * 2 + (leaf & 1)
        parent = (leaf >> 5 & 1) * 4 + (leaf >> 3 & 1) * 2 + (leaf >> 1 & 1)
        here = lane == odd * 8 + parent
        slots = pl.ds(pl.multiple_of(leaf * P_CAP, P_CAP), P_CAP)
        live = lane_row < counts_ref[leaf]
        place = [jnp.broadcast_to(offsets_ref[s : s + 1, slots], (8, P_CAP)) for s in range(3)]
        force = [
            jnp.broadcast_to(jnp.where(live, forces_ref[s : s + 1, slots], 0.0), (8, P_CAP))
            for s in range(3)
        ]
        for first in range(0, points, 8):
            apart = [targets_ref[s * points + first : s * points + first + 8] - place[s] for s in range(3)]
            inverse = lax.rsqrt(apart[0] * apart[0] + apart[1] * apart[1] + apart[2] * apart[2])
            projected = apart[0] * force[0] + apart[1] * force[1] + apart[2] * force[2]
            scaled = projected * inverse * inverse
            for s in range(3):
                value = (force[s] + apart[s] * scaled) * inverse
                summed = jnp.sum(value, axis=1, keepdims=True)
                rows = slice(s * points + first, s * points + first + 8)
                check[rows] = jnp.where(here, summed, check[rows])
        return carry

    lax.fori_loop(0, LEAF_DEV, one_leaf, 0, unroll=2)

    potentials = jnp.transpose(check[...])[:LEAF_DEV, :NCOEF]
    load(3).wait()
    load(4).wait()
    leaf_density = product(potentials, *halves(uc2ue_ref[...]))
    mid_density = jnp.zeros((8, NCOEF), f32)
    for o in range(8):
        pltpu.make_async_copy(m2m_hbm.at[o], m2m.at[o], arrivals.at[o]).wait()
        high, low = halves(m2m[o])
        m2m_high[o] = high
        m2m_low[o] = low
        mid_density += product(leaf_density[8 * o : 8 * o + 8], high, low)
    shrink = halves(compress_ref[...])
    rounded = product(jnp.concatenate([leaf_density, mid_density], axis=0), *shrink, contracted=1).astype(bf16)
    row = lax.broadcasted_iota(jnp.int32, (48, 144), 0)
    col = lax.broadcasted_iota(jnp.int32, (48, 144), 1)
    half = jnp.where(col >= 72, 1, 0)
    odd = half * 4 + (row >> 2 & 1) * 2 + (row & 1)
    parent = (row >> 5) * 4 + (row >> 3 & 1) * 2 + (row >> 1 & 1)
    place = (row & 15) + jnp.where((row & 15) < 4, half * 4 + LEAF_DEV, 2 * LEAF_DEV)
    wanted = jnp.where((row >> 4) == 1, place, odd * 8 + parent)
    order = jnp.where(col - 72 * half == wanted, 1.0, 0.0).astype(bf16)
    nothing = jnp.zeros((72, RANK), bf16)
    pairs = jnp.concatenate(
        [jnp.concatenate([rounded, nothing], axis=1), jnp.concatenate([nothing, rounded], axis=1)], axis=0
    )
    block_ref[...] = jnp.dot(order, pairs, preferred_element_type=f32).astype(bf16)

    pl.semaphore_wait(barrier, peers - 1)
    near_numbers = [number for number in range(12) if number != 4]
    for number in near_numbers:
        near_copy(number).start()
    nearby[1, own] = block_ref[...]

    own_density = jnp.zeros((8, NCOEF), f32)
    for o in range(8):
        child = jnp.broadcast_to(mid_density[o : o + 1], (8, NCOEF))
        own_density += product(child, m2m_high[o], m2m_low[o])
    lifted = product(own_density, m2m_high[octant], m2m_low[octant])
    shrunk = product(jnp.concatenate([own_density, lifted], axis=0), *shrink, contracted=1)
    small_ref[...] = jnp.concatenate([shrunk[0:1].astype(bf16).astype(f32), shrunk[8:9]], axis=1)

    def send_small(k, carry):
        small_copy(k, me).start()
        return carry

    lax.fori_loop(1, peers, send_small, 0)
    every[pl.ds(me, 1)] = small_ref[...]

    load(5).wait()
    directions = stored_ref.shape[2]

    def turn(j, carry):
        pairs = jnp.concatenate([stored_ref[j], stored_ref[j + HALF]], axis=0)
        operator_rows[pl.ds(j, directions, stride=PITCH), :] = jnp.transpose(pairs).astype(f32)
        return carry

    lax.fori_loop(0, HALF, turn, 0, unroll=4)

    row = lax.broadcasted_iota(jnp.int32, (224, 256), 0)
    col = lax.broadcasted_iota(jnp.int32, (224, 256), 1)
    step_y = (row >> 5) - 3
    slot = ((row >> 4) & 1) * 4 + (col >> 6)
    step_z = jnp.where(slot < 4, slot - 3 + 3 * (slot >> 1), slot - 5)
    usable = slot < 7

    def chosen(side_bits, target, source, step, bit):
        target = (bit << side_bits) + target
        return (source - target == step) & (jnp.abs((source >> 1) - (target >> 1)) <= 1)

    leaf_select = (
        usable
        & chosen(2, (row >> 2) & 3, (((col >> 5) & 1) << 2) + ((col >> 2) & 3), step_y, y_bit)
        & chosen(2, row & 3, (((col >> 4) & 1) << 2) + (col & 3), step_z, z_bit)
    )
    leaf_select = jnp.where(leaf_select, 1.0, 0.0).astype(bf16)
    mid_base = (
        usable
        & ((row & 15) < 4)
        & ((col & 15) < 4)
        & chosen(1, (row >> 1) & 1, (((col >> 5) & 1) << 1) + ((col >> 1) & 1), step_y, y_bit)
        & chosen(1, row & 1, (((col >> 4) & 1) << 1) + (col & 1), step_z, z_bit)
    )
    mid_select = jnp.where(mid_base, 1.0, 0.0).astype(bf16)
    on_diagonal = (lax.broadcasted_iota(jnp.int32, (256, 256), 0) >> 6) == (
        (lax.broadcasted_iota(jnp.int32, (256, 256), 1) >> 5) & 3
    )

    blank = jnp.zeros((14, 16, 256), bf16)
    leaf_rows[0] = blank
    leaf_rows[9] = blank
    mid_rows[0] = blank
    mid_rows[7] = blank

    blank = jnp.zeros((14, 16, 256), bf16)
    leaf_rows[0] = blank
    leaf_rows[9] = blank
    mid_rows[0] = blank
    mid_rows[7] = blank
    for number in near_numbers:
        near_copy(number, True).wait_recv()

    for c in range(3):
        inside = (column + c >= 1) & (column + c <= columns_x)
        diagonal = jnp.where(on_diagonal & inside, 1.0, 0.0).astype(bf16)
        for first in range(0, 48, 16):
            if (c, first) in ((0, 0), (2, 32)):
                continue
            stack = nearby[c, :, first : first + 16, :].reshape(64, 128)
            for lx in range(2):
                low = stack[:, RANK * lx : RANK * lx + HALF]
                high = stack[:, RANK * lx + HALF : RANK * lx + RANK]
                wide = jnp.concatenate([low] * 4 + [high] * 4, axis=1)
                sources = jnp.concatenate([wide] * 4, axis=0) * diagonal
                if first == 16:
                    got = jnp.dot(mid_select, sources, preferred_element_type=f32)
                    mid_rows[2 * c + lx + 1] = got.astype(bf16).reshape(14, 16, 256)
                else:
                    got = jnp.dot(leaf_select, sources, preferred_element_type=f32)
                    leaf_rows[4 * c + first // 16 + lx - 1] = got.astype(bf16).reshape(14, 16, 256)

    bases = {-3: 0, -2: 49, 2: 218, 3: 267}
    first_direction = 0
    odd_target = (lax.broadcasted_iota(jnp.int32, (192, 128), 0) >> 4) & 1
    total = jnp.zeros((192, 128), f32)
    for u in range(7):
        part = jnp.zeros((192, 128), f32)
        for v in range(7):

            def operand(quads):
                rows = []
                for lanes in (slice(0, 128), slice(128, 256)):
                    for ref, count in ((leaf_rows, 4), (mid_rows, 2)):
                        pieces = [
                            ref[u : u + count, 2 * v + quad, :, lanes].reshape(16 * count, 128)
                            for quad in quads
                        ]
                        rows.append(jnp.concatenate(pieces, axis=1))
                return jnp.concatenate(rows, axis=0)

            def operators(steps):
                rows = [operator_rows[(first_direction + k) * PITCH : (first_direction + k) * PITCH + HALF] for k in steps]
                return jnp.concatenate(rows, axis=0).astype(bf16)

            if 2 <= u <= 4 and 2 <= v <= 4:
                part += jnp.dot(operand((0,)), operators((0, 1, 2, 3)), preferred_element_type=f32)
                first_direction += 4
            else:
                part += jnp.dot(operand((0, 1)), operators((0, 1, 5, 6, 2, 3, 4, 4)), preferred_element_type=f32)
                first_direction += 7
        if u == 0:
            part = jnp.where(odd_target == 1, part, 0.0)
        if u == 6:
            part = jnp.where(odd_target == 0, part, 0.0)
        total += part
    total = total[:96, :RANK] + total[96:, RANK:]
    packed_ref[1:5] = total[64:68]
    packed_ref[5:9] = total[80:84]
    packed_ref[9:73] = total[:64]

    def small_arrived(k, carry):
        small_copy(k, (me - k + peers) % peers).wait_recv()
        return carry

    lax.fori_loop(1, peers, small_arrived, 0)

    own_total = jnp.zeros((1, RANK), f32)
    for u in (-3, -2, 2, 3):
        other = column + u
        good = (other >= 0) & (other < columns_x)
        if u == -3:
            good = good & (column % 2 == 1)
        if u == 3:
            good = good & (column % 2 == 0)
        wrapped = (other + 4 * columns_x) % columns_x
        part = jnp.zeros((1, RANK), f32)
        for sy in range(2):
            for sz in range(2):
                direction = bases[u] + (sy - y_bit + 3) * 7 + (sz - z_bit + 3)
                source = every[pl.ds(wrapped * 4 + sy * 2 + sz, 1)].astype(bf16)
                rows = pl.ds(pl.multiple_of(direction * PITCH, 8), HALF)
                operator = operator_rows[rows].astype(bf16)
                part += jnp.dot(source[:, :HALF], operator[:, :RANK], preferred_element_type=f32)
                part += jnp.dot(source[:, HALF:RANK], operator[:, RANK:], preferred_element_type=f32)
        own_total += jnp.where(good, part, 0.0)
    packed_ref[0:1] = own_total

    load(6).wait()
    padded[...] = jnp.zeros_like(padded)
    for r in range(root_count):
        padded[root_count + r : root_count + r + 1] = jnp.sum(every[8 * r : 8 * r + 8], axis=0, keepdims=True)
    found = jnp.zeros((root_count, RANK), f32)
    for k in range(2 * root_count - 1):
        distance = k - (root_count - 1)
        if abs(distance) >= 2:
            start = root_count + distance
            source = padded[start : start + root_count, :][:, RANK:].astype(bf16)
            found += jnp.dot(source, root_ref[k], preferred_element_type=f32)
    packed_ref[FIRST_ROOT : FIRST_ROOT + root_count] = found

    for number in near_numbers:
        near_copy(number).wait_send()

    def small_sent(k, carry):
        small_copy(k, me).wait_send()
        return carry

    lax.fori_loop(1, peers, small_sent, 0)


def finish_kernel(packed_ref, boxes_ref, roots_ref):
    boxes_ref[...] = jnp.transpose(packed_ref[...])[:, : LEAF_DEV + 9]
    roots_ref[...] = packed_ref[FIRST_ROOT : FIRST_ROOT + roots_ref.shape[0]]


def body(offsets, forces, counts, uc2ue, m2m_ops, compress, m2l_ops, root_ops):
    f32, bf16 = jnp.float32, jnp.bfloat16
    peers = lax.axis_size("morton")
    root_count = peers // 8
    vmem, anywhere = pl.BlockSpec(memory_space=pltpu.VMEM), pl.BlockSpec(memory_space=pl.ANY)
    targets = np.repeat(surface_points().reshape(NCOEF, 1), P_CAP, axis=1)
    stored = jnp.transpose(m2l_ops, (1, 2, 0))
    directions = m2l_ops.shape[0]
    packed = pl.pallas_call(
        functools.partial(solver_kernel, peers),
        out_shape=jax.ShapeDtypeStruct((FIRST_ROOT + (root_count + 7) // 8 * 8, RANK), f32),
        in_specs=[pl.BlockSpec(memory_space=pltpu.SMEM)] + [anywhere] * 8,
        out_specs=vmem,
        scratch_shapes=[
            pltpu.VMEM(offsets.shape, f32),
            pltpu.VMEM(forces.shape, f32),
            pltpu.VMEM(targets.shape, f32),
            pltpu.VMEM(uc2ue.shape, f32),
            pltpu.VMEM((RANK, NCOEF), f32),
            pltpu.VMEM(m2m_ops.shape, f32),
            pltpu.VMEM(m2m_ops.shape, bf16),
            pltpu.VMEM(m2m_ops.shape, bf16),
            pltpu.VMEM(stored.shape, bf16),
            pltpu.VMEM(root_ops.shape, bf16),
            pltpu.VMEM((512, 128), f32),
            pltpu.VMEM((1, 128), f32),
            pltpu.VMEM((48, 128), bf16),
            pltpu.VMEM((peers, 128), f32),
            pltpu.VMEM((3, 4, 48, 128), bf16),
            pltpu.VMEM((10, 14, 16, 256), bf16),
            pltpu.VMEM((8, 14, 16, 256), bf16),
            pltpu.VMEM((directions * PITCH, 2 * RANK), f32),
            pltpu.VMEM((3 * root_count, 128), f32),
            pltpu.SemaphoreType.DMA((7,)),
            pltpu.SemaphoreType.DMA((8,)),
            pltpu.SemaphoreType.DMA((peers,)),
            pltpu.SemaphoreType.DMA((peers,)),
            pltpu.SemaphoreType.DMA((12,)),
            pltpu.SemaphoreType.DMA((12,)),
        ],
        compiler_params=pltpu.CompilerParams(collective_id=0, has_side_effects=True, vmem_limit_bytes=60 << 20),
    )(counts, offsets, forces, jnp.asarray(targets, dtype=f32), uc2ue, compress.T, m2m_ops, stored, root_ops)
    boxes, roots = pl.pallas_call(
        finish_kernel,
        out_shape=(
            jax.ShapeDtypeStruct((RANK, LEAF_DEV + 9), f32),
            jax.ShapeDtypeStruct((root_count, RANK), f32),
        ),
        in_specs=[vmem],
        out_specs=(vmem, vmem),
    )(packed)
    return jnp.transpose(boxes), roots


def solution(mesh):
    placed = (P(None, "morton"), P(None, "morton"), P("morton"), P(), P(), P(), P(), P())
    return jax.shard_map(
        body, mesh=mesh, in_specs=placed, out_specs=(P("morton", None), P()), check_vma=False
    )
```

time: 36.1 us -> 28.1 us (0.78)
  Pallas kernels: 32.5 us -> 27.3 us
  local copies, waits for them, and re-layouts: 2.74 us -> 0 us
    pallas_call x2, Pallas kernels: 32.5 us -> 27.3 us  [the longest x1 25.8 us: body(): pl.pallas_call(functools.partial(solver_kernel, peers), out_shape=jax.Sha...]
    pallas_call x1 -> x0, local copies, waits for them, and re-layouts: 1.48 us -> none  [far_field(): pl.pallas_call(functools.partial(exchange_kernel, peers), out_shape=(jax....]
    unnamed x1 -> x0, local copies, waits for them, and re-layouts: 1.26 us -> none
where the time goes in v2:
time: 28.1 us; the launch traced here: 27.9 us
  Pallas kernels  27.3 us (97%)
  between operations  0.64 us (2%)
    pallas_call x1, Pallas kernels, body(): pl.pallas_call(functools.partial(solver_kernel, peers), out_shape=jax.Sha...  25.8 us
    pallas_call x1, Pallas kernels, body(): pl.pallas_call(finish_kernel, out_shape=(jax.ShapeDtypeStruct((RANK, LEAF...  1.49 us

profile of v2, /device:TPU:0, one launch (start us, length us, event | category | flops | bytes accessed | tf_op | source)
XLA Modules:
  0.0 27.9 jit_solution(2262190046166961765)
XLA Ops:
  0.6 25.8 %shard_map.104.packed_ref = f32[88,64]{1,0:T(8,128)} custom-call(s32[64]{0:T(128)} %counts_ref.1, f32[3,8192]{1,0:T(4,128)} %offsets_hbm.1, f32[3,8192]{1,0:T(4,128)} %forces_hbm.1, f32[456,128]{1,0:T(8,128)} %constant.2.clone.targets_hbm, f32[456,456]{1,0:T(8,128)} %uc2ue_hbm.1, f32[64,456]{1,0:T(8,128)} %bitcast.4, f32[8,456,456]{2,1,0:T(8,128)} %m2m_hbm.1, ...), custom_call_target="tpu_custom_call" | custom-call | tf_op jit(solution)/shard_map/pallas_call | solution.py:371
  26.4 1.5 %shard_map.105 = (f32[64,73]{1,0:T(8,128)}, f32[4,64]{1,0:T(4,128)}) custom-call(f32[88,64]{1,0:T(8,128)} %shard_map.104.packed_ref), custom_call_target="tpu_custom_call" | custom-call | tf_op jit(solution)/shard_map/pallas_call | solution.py:405

commit v3 on v2

--- a/solution.py
+++ b/solution.py
@@ -19,23 +19,19 @@
 
 
 check_radius = 1.475
+LEAF_PITCH = LEAF_DEV + 8
+APART = tuple(3 * SURF_ORDER * s for s in range(3))
+SQUARE = tuple(first + SURF_ORDER for first in APART)
+ALONG = tuple(first + 2 * SURF_ORDER for first in APART)
+FORCE = 9 * SURF_ORDER
 MESH = pl.DeviceIdType.MESH
 
 
-def surface_points():
-    tick_values = np.linspace(-1.0, 1.0, SURF_ORDER)
-    chosen = []
-    for along_x in range(SURF_ORDER):
-        for along_y in range(SURF_ORDER):
-            for along_z in range(SURF_ORDER):
-                if (
-                    min(along_x, along_y, along_z) == 0
-                    or max(along_x, along_y, along_z) == SURF_ORDER - 1
-                ):
-                    chosen.append(
-                        (tick_values[along_x], tick_values[along_y], tick_values[along_z])
-                    )
-    return check_radius * np.array(chosen).T
+def surface_grid():
+    order = range(SURF_ORDER)
+    ends = (0, SURF_ORDER - 1)
+    surface = [(i, j, k) for i in order for j in order for k in order if i in ends or j in ends or k in ends]
+    return surface, [float(np.float32(check_radius * tick)) for tick in np.linspace(-1.0, 1.0, SURF_ORDER)]
 
 
 def two_parts(value):
@@ -57,13 +53,15 @@
     return high.astype(jnp.bfloat16), low.astype(jnp.bfloat16)
 
 
-def solver_kernel(peers, counts_ref, offsets_hbm, forces_hbm, targets_hbm, uc2ue_hbm, compress_hbm, m2m_hbm, stored_hbm, root_hbm,
+def solver_kernel(peers, counts_ref, offsets_hbm, forces_hbm, uc2ue_hbm, compress_hbm, m2m_hbm, stored_hbm, root_hbm,
                   packed_ref,
-                  offsets_ref, forces_ref, targets_ref, uc2ue_ref, compress_ref, m2m, m2m_high, m2m_low, stored_ref, root_ref, check,
+                  offsets_ref, forces_ref, uc2ue_ref, compress_ref, m2m, m2m_high, m2m_low, stored_ref, root_ref, check,
+                  slots_by_leaf, table, sums,
                   small_ref, block_ref, every, nearby, leaf_rows, mid_rows, operator_rows, padded,
                   loads, arrivals, send_all, recv_all, send_near, recv_near):
     f32, bf16 = jnp.float32, jnp.bfloat16
-    points = NCOEF // 3
+    surface, ticks = surface_grid()
+    points = len(surface)
     me = lax.axis_index("morton")
     columns_x, root_count = peers // 4, peers // 8
     column, y_bit, z_bit = me // 4, me // 2 % 2, me % 2
@@ -72,10 +70,9 @@
     wholes = (
         (offsets_hbm, offsets_ref),
         (forces_hbm, forces_ref),
-        (targets_hbm, targets_ref),
+        (stored_hbm, stored_ref),
         (uc2ue_hbm, uc2ue_ref),
         (compress_hbm, compress_ref),
-        (stored_hbm, stored_ref),
         (root_hbm, root_ref),
     )
 
@@ -86,8 +83,7 @@
         load(number).start()
     for o in range(8):
         pltpu.make_async_copy(m2m_hbm.at[o], m2m.at[o], arrivals.at[o]).start()
-    for number in range(5, 7):
-        load(number).start()
+    load(5).start()
 
     barrier = pltpu.get_barrier_semaphore()
 
@@ -115,38 +111,77 @@
             src_ref=small_ref, dst_ref=every.at[pl.ds(slot, 1)], send_sem=send_all.at[k],
             recv_sem=recv_all.at[k], device_id=((me + k) % peers,), device_id_type=MESH)
 
-    for number in range(3):
-        load(number).wait()
-    check[...] = jnp.zeros_like(check)
-    lane = lax.broadcasted_iota(jnp.int32, (8, 128), 1)
-    lane_row = lax.broadcasted_iota(jnp.int32, (1, 128), 1)
-
-    def one_leaf(leaf, carry):
+    sums[...] = jnp.zeros_like(sums)
+    check[NCOEF:] = jnp.zeros((check.shape[0] - NCOEF, 128), f32)
+    load(0).wait()
+    load(1).wait()
+    lane_row = lax.broadcasted_iota(jnp.int32, (1, P_CAP), 1)
+
+    def place(leaf, carry):
         odd = (leaf >> 4 & 1) * 4 + (leaf >> 2 & 1) * 2 + (leaf & 1)
         parent = (leaf >> 5 & 1) * 4 + (leaf >> 3 & 1) * 2 + (leaf >> 1 & 1)
-        here = lane == odd * 8 + parent
         slots = pl.ds(pl.multiple_of(leaf * P_CAP, P_CAP), P_CAP)
         live = lane_row < counts_ref[leaf]
-        place = [jnp.broadcast_to(offsets_ref[s : s + 1, slots], (8, P_CAP)) for s in range(3)]
-        force = [
-            jnp.broadcast_to(jnp.where(live, forces_ref[s : s + 1, slots], 0.0), (8, P_CAP))
-            for s in range(3)
-        ]
-        for first in range(0, points, 8):
-            apart = [targets_ref[s * points + first : s * points + first + 8] - place[s] for s in range(3)]
-            inverse = lax.rsqrt(apart[0] * apart[0] + apart[1] * apart[1] + apart[2] * apart[2])
-            projected = apart[0] * force[0] + apart[1] * force[1] + apart[2] * force[2]
-            scaled = projected * inverse * inverse
+        slots_by_leaf[pl.ds(odd * 8 + parent, 3, stride=LEAF_PITCH), :] = offsets_ref[:, slots]
+        slots_by_leaf[pl.ds(3 * LEAF_PITCH + odd * 8 + parent, 3, stride=LEAF_PITCH), :] = jnp.where(
+            live, forces_ref[:, slots], 0.0
+        )
+        return carry
+
+    lax.fori_loop(0, LEAF_DEV, place, 0, unroll=8)
+    for s in range(6):
+        leaves = slots_by_leaf[s * LEAF_PITCH : s * LEAF_PITCH + LEAF_DEV]
+        leaves = jnp.concatenate([leaves[:, : P_CAP // 2], leaves[:, P_CAP // 2 :]], axis=0)
+        table[:, s if s < 3 else FORCE + s - 3] = jnp.transpose(leaves).reshape(8, 8, 128)
+
+    def prepare(block, carry):
+        place = [table[block, s] for s in range(3)]
+        force = [table[block, FORCE + s] for s in range(3)]
+        for s in range(3):
+            for i in range(SURF_ORDER):
+                apart = ticks[i] - place[s]
+                table[block, APART[s] + i] = apart
+                table[block, SQUARE[s] + i] = apart * apart
+                table[block, ALONG[s] + i] = apart * force[s]
+        return carry
+
+    lax.fori_loop(0, 8, prepare, 0)
+    load(2).wait()
+    directions = stored_ref.shape[2]
+
+    def turn(j):
+        pairs = jnp.concatenate([stored_ref[j], stored_ref[j + HALF]], axis=0)
+        operator_rows[pl.ds(j, directions, stride=PITCH), :] = jnp.transpose(pairs).astype(f32)
+
+    def two_blocks(step, carry):
+        blocks = (2 * step, 2 * step + 1)
+        force = [[table[block, FORCE + s] for s in range(3)] for block in blocks]
+        column_now = None
+        for q, (i, j, k) in enumerate(surface):
+            if q % (points // 8) == 0:
+                turn(8 * step + q // (points // 8))
+            if (i, j) != column_now:
+                column_now = (i, j)
+                square = [table[block, SQUARE[0] + i] + table[block, SQUARE[1] + j] for block in blocks]
+                along = [table[block, ALONG[0] + i] + table[block, ALONG[1] + j] for block in blocks]
+            values = [[], [], []]
+            for n, block in enumerate(blocks):
+                inverse = lax.rsqrt(square[n] + table[block, SQUARE[2] + k])
+                projected = along[n] + table[block, ALONG[2] + k]
+                scaled = projected * (inverse * inverse)
+                for s, tick in enumerate((i, j, k)):
+                    values[s].append((force[n][s] + table[block, APART[s] + tick] * scaled) * inverse)
             for s in range(3):
-                value = (force[s] + apart[s] * scaled) * inverse
-                summed = jnp.sum(value, axis=1, keepdims=True)
-                rows = slice(s * points + first, s * points + first + 8)
-                check[rows] = jnp.where(here, summed, check[rows])
-        return carry
-
-    lax.fori_loop(0, LEAF_DEV, one_leaf, 0, unroll=2)
-
-    potentials = jnp.transpose(check[...])[:LEAF_DEV, :NCOEF]
+                rows = slice((s * points + q) * 8, (s * points + q) * 8 + 8)
+                sums[rows] += values[s][0] + values[s][1]
+        return carry
+
+    lax.fori_loop(0, 4, two_blocks, 0)
+    for first in range(0, NCOEF, 8):
+        rows = [sums[pl.ds(8 * first + r, 8, stride=8), :] for r in range(8)]
+        check[first : first + 8] = ((rows[0] + rows[1]) + (rows[2] + rows[3])) + ((rows[4] + rows[5]) + (rows[6] + rows[7]))
+    potentials = jnp.transpose(check[...])[:, :NCOEF]
+    potentials = potentials[:LEAF_DEV] + potentials[LEAF_DEV:]
     load(3).wait()
     load(4).wait()
     leaf_density = product(potentials, *halves(uc2ue_ref[...]))
@@ -194,16 +229,6 @@
     lax.fori_loop(1, peers, send_small, 0)
     every[pl.ds(me, 1)] = small_ref[...]
 
-    load(5).wait()
-    directions = stored_ref.shape[2]
-
-    def turn(j, carry):
-        pairs = jnp.concatenate([stored_ref[j], stored_ref[j + HALF]], axis=0)
-        operator_rows[pl.ds(j, directions, stride=PITCH), :] = jnp.transpose(pairs).astype(f32)
-        return carry
-
-    lax.fori_loop(0, HALF, turn, 0, unroll=4)
-
     row = lax.broadcasted_iota(jnp.int32, (224, 256), 0)
     col = lax.broadcasted_iota(jnp.int32, (224, 256), 1)
     step_y = (row >> 5) - 3
@@ -332,7 +357,7 @@
         own_total += jnp.where(good, part, 0.0)
     packed_ref[0:1] = own_total
 
-    load(6).wait()
+    load(5).wait()
     padded[...] = jnp.zeros_like(padded)
     for r in range(root_count):
         padded[root_count + r : root_count + r + 1] = jnp.sum(every[8 * r : 8 * r + 8], axis=0, keepdims=True)
@@ -365,18 +390,16 @@
     peers = lax.axis_size("morton")
     root_count = peers // 8
     vmem, anywhere = pl.BlockSpec(memory_space=pltpu.VMEM), pl.BlockSpec(memory_space=pl.ANY)
-    targets = np.repeat(surface_points().reshape(NCOEF, 1), P_CAP, axis=1)
     stored = jnp.transpose(m2l_ops, (1, 2, 0))
     directions = m2l_ops.shape[0]
     packed = pl.pallas_call(
         functools.partial(solver_kernel, peers),
         out_shape=jax.ShapeDtypeStruct((FIRST_ROOT + (root_count + 7) // 8 * 8, RANK), f32),
-        in_specs=[pl.BlockSpec(memory_space=pltpu.SMEM)] + [anywhere] * 8,
+        in_specs=[pl.BlockSpec(memory_space=pltpu.SMEM)] + [anywhere] * 7,
         out_specs=vmem,
         scratch_shapes=[
             pltpu.VMEM(offsets.shape, f32),
             pltpu.VMEM(forces.shape, f32),
-            pltpu.VMEM(targets.shape, f32),
             pltpu.VMEM(uc2ue.shape, f32),
             pltpu.VMEM((RANK, NCOEF), f32),
             pltpu.VMEM(m2m_ops.shape, f32),
@@ -385,6 +408,9 @@
             pltpu.VMEM(stored.shape, bf16),
             pltpu.VMEM(root_ops.shape, bf16),
             pltpu.VMEM((512, 128), f32),
+            pltpu.VMEM((6 * LEAF_PITCH, P_CAP), f32),
+            pltpu.VMEM((8, FORCE + 3, 8, 128), f32),
+            pltpu.VMEM((8 * NCOEF, 128), f32),
             pltpu.VMEM((1, 128), f32),
             pltpu.VMEM((48, 128), bf16),
             pltpu.VMEM((peers, 128), f32),
@@ -393,7 +419,7 @@
             pltpu.VMEM((8, 14, 16, 256), bf16),
             pltpu.VMEM((directions * PITCH, 2 * RANK), f32),
             pltpu.VMEM((3 * root_count, 128), f32),
-            pltpu.SemaphoreType.DMA((7,)),
+            pltpu.SemaphoreType.DMA((6,)),
             pltpu.SemaphoreType.DMA((8,)),
             pltpu.SemaphoreType.DMA((peers,)),
             pltpu.SemaphoreType.DMA((peers,)),
@@ -401,7 +427,7 @@
             pltpu.SemaphoreType.DMA((12,)),
         ],
         compiler_params=pltpu.CompilerParams(collective_id=0, has_side_effects=True, vmem_limit_bytes=60 << 20),
-    )(counts, offsets, forces, jnp.asarray(targets, dtype=f32), uc2ue, compress.T, m2m_ops, stored, root_ops)
+    )(counts, offsets, forces, uc2ue, compress.T, m2m_ops, stored, root_ops)
     boxes, roots = pl.pallas_call(
         finish_kernel,
         out_shape=(
@@ -410,6 +436,7 @@
         ),
         in_specs=[vmem],
         out_specs=(vmem, vmem),
+        compiler_params=pltpu.CompilerParams(vmem_limit_bytes=1 << 20),
     )(packed)
     return jnp.transpose(boxes), roots
 

time: 28.1 us -> 26.7 us (0.950)
  Pallas kernels: 27.3 us -> 25.1 us
  local copies, waits for them, and re-layouts: 0 us -> 0.78 us
    pallas_call x1, Pallas kernels: 25.8 us -> 24.4 us  [body(): pl.pallas_call(functools.partial(solver_kernel, peers), out_shape=jax.Sha...]
    pallas_call x1, Pallas kernels: 1.49 us -> 0.7 us  [body(): pl.pallas_call(finish_kernel, out_shape=(jax.ShapeDtypeStruct((RANK, LEAF...]
    unnamed x0 -> x2, local copies, waits for them, and re-layouts: none -> 0.78 us
where the time goes in v3:
time: 26.7 us; the launch traced here: 26.6 us
  Pallas kernels  25.1 us (94%)
  local copies, waits for them, and re-layouts  0.78 us (3%)
  between operations  0.65 us (2%)
    pallas_call x1, Pallas kernels, body(): pl.pallas_call(functools.partial(solver_kernel, peers), out_shape=jax.Sha...  24.4 us
    unnamed x2, local copies, waits for them, and re-layouts  0.78 us
    pallas_call x1, Pallas kernels, body(): pl.pallas_call(finish_kernel, out_shape=(jax.ShapeDtypeStruct((RANK, LEAF...  0.7 us

profile of v3, /device:TPU:0, one launch (start us, length us, event | category | flops | bytes accessed | tf_op | source)
XLA Modules:
  0.0 26.6 jit_solution(4084928770014466404)
XLA Ops:
  0.6 24.4 %shard_map.95.packed_ref = f32[88,64]{1,0:T(8,128)} custom-call(s32[64]{0:T(128)} %counts_ref.1, f32[3,8192]{1,0:T(4,128)} %offsets_hbm.1, f32[3,8192]{1,0:T(4,128)} %forces_hbm.1, f32[456,456]{1,0:T(8,128)} %uc2ue_hbm.1, f32[64,456]{1,0:T(8,128)} %bitcast.4, f32[8,456,456]{2,1,0:T(8,128)} %m2m_hbm.1, bf16[64,64,316]{2,1,0:T(8,128)(2,1)} %bitcast.3, ...), custom_call_target="tpu_custom_call" | custom-call | tf_op jit(solution)/shard_map/pallas_call | solution.py:395
  25.1 0.0 copy-start
  25.1 0.8 %copy-done = f32[88,64]{1,0:T(8,128)S(1)} copy-done((f32[88,64]{1,0:T(8,128)S(1)}, f32[88,64]{1,0:T(8,128)}, u32[]{:S(2)}) %copy-start) | copy-done | bytes 22552
  25.9 0.7 %shard_map.96 = (f32[64,73]{1,0:T(8,128)}, f32[4,64]{1,0:T(4,128)}) custom-call(f32[88,64]{1,0:T(8,128)S(1)} %copy-done), custom_call_target="tpu_custom_call" | custom-call | tf_op jit(solution)/shard_map/pallas_call | solution.py:431
Async XLA Ops:
  25.1 0.8 %copy-start = (f32[88,64]{1,0:T(8,128)S(1)}, f32[88,64]{1,0:T(8,128)}, u32[]{:S(2)}) copy-start(f32[88,64]{1,0:T(8,128)} %shard_map.95.packed_ref) | copy-start | bytes 67588

commit v4 on v3

--- a/solution.py
+++ b/solution.py
@@ -39,13 +39,24 @@
     return high, value - high
 
 
-def product(value, high, low, contracted=0):
+def product(value, high, low):
     rows = value.shape[0]
-    parts = jnp.concatenate(two_parts(value), axis=0).astype(jnp.bfloat16)
-    dims = (((1,), (contracted,)), ((), ()))
-    both = lax.dot_general(parts, low, dims, preferred_element_type=jnp.float32)
-    both += lax.dot_general(parts, high, dims, preferred_element_type=jnp.float32)
+    parts = two_bf16(value)
+    both = jnp.dot(parts, low, preferred_element_type=jnp.float32)
+    both += jnp.dot(parts, high, preferred_element_type=jnp.float32)
     return both[:rows] + both[rows:]
+
+
+def two_bf16(value):
+    return jnp.concatenate(two_parts(value), axis=0).astype(jnp.bfloat16)
+
+
+def shrunk(parts, shrink):
+    dims = (((1,), (1,)), ((), ()))
+    both = lax.dot_general(parts, shrink, dims, preferred_element_type=jnp.float32)
+    rows, rank = parts.shape[0] // 2, shrink.shape[0] // 2
+    both = both[:rows] + both[rows:]
+    return both[:, :rank] + both[:, rank:]
 
 
 def halves(matrix):
@@ -70,46 +81,63 @@
     wholes = (
         (offsets_hbm, offsets_ref),
         (forces_hbm, forces_ref),
-        (stored_hbm, stored_ref),
         (uc2ue_hbm, uc2ue_ref),
         (compress_hbm, compress_ref),
+        (stored_hbm, stored_ref),
         (root_hbm, root_ref),
     )
 
     def load(number):
         return pltpu.make_async_copy(*wholes[number], loads.at[number])
 
-    for number in range(5):
+    for number in range(4):
         load(number).start()
     for o in range(8):
         pltpu.make_async_copy(m2m_hbm.at[o], m2m.at[o], arrivals.at[o]).start()
+    load(4).start()
     load(5).start()
 
+    def around(k):
+        return jnp.where(me + k >= peers, me + k - peers, me + k)
+
     barrier = pltpu.get_barrier_semaphore()
 
     def greet(k, carry):
-        pl.semaphore_signal(barrier, inc=1, device_id=((me + k) % peers,), device_id_type=MESH)
-        return carry
-
-    lax.fori_loop(1, peers, greet, 0)
+        pl.semaphore_signal(barrier, inc=1, device_id=(around(k),), device_id_type=MESH)
+        return carry
+
+    lax.fori_loop(1, peers, greet, 0, unroll=4)
 
     parts = {-1: (0, 32), 0: (0, 48), 1: (16, 48)}
 
-    def near_copy(number, arriving=False):
+    def near_copy(number):
         dc, flip_y, flip_z = number // 4 - 1, number // 2 % 2, number % 2
         other = (y_bit + flip_y) % 2 * 2 + (z_bit + flip_z) % 2
         peer = (column + dc + columns_x) % columns_x * 4 + other
         first, last = parts[dc]
         return pltpu.make_async_remote_copy(
             src_ref=block_ref.at[first:last],
-            dst_ref=nearby.at[1 - dc, other if arriving else own, first:last],
-            send_sem=send_near.at[number], recv_sem=recv_near.at[number],
+            dst_ref=nearby.at[1 - dc, own, first:last],
+            send_sem=send_near.at[1 - dc], recv_sem=recv_near.at[1 - dc],
             device_id=(peer,), device_id_type=MESH)
 
-    def small_copy(k, slot):
+    def near_whole(c):
+        count, (first, last) = (3 if c == 1 else 4), parts[1 - c]
+        space = nearby.at[c, 0:count, first:last]
         return pltpu.make_async_remote_copy(
-            src_ref=small_ref, dst_ref=every.at[pl.ds(slot, 1)], send_sem=send_all.at[k],
-            recv_sem=recv_all.at[k], device_id=((me + k) % peers,), device_id_type=MESH)
+            src_ref=space, dst_ref=space, send_sem=send_near.at[c], recv_sem=recv_near.at[c],
+            device_id=(me,), device_id_type=MESH)
+
+    def small_copy(k):
+        return pltpu.make_async_remote_copy(
+            src_ref=small_ref, dst_ref=every.at[pl.ds(me, 1)], send_sem=send_all, recv_sem=recv_all,
+            device_id=(around(k),), device_id_type=MESH)
+
+    def small_whole():
+        space = every.at[0 : peers - 1]
+        return pltpu.make_async_remote_copy(
+            src_ref=space, dst_ref=space, send_sem=send_all, recv_sem=recv_all,
+            device_id=(me,), device_id_type=MESH)
 
     sums[...] = jnp.zeros_like(sums)
     check[NCOEF:] = jnp.zeros((check.shape[0] - NCOEF, 128), f32)
@@ -146,20 +174,11 @@
         return carry
 
     lax.fori_loop(0, 8, prepare, 0)
-    load(2).wait()
-    directions = stored_ref.shape[2]
-
-    def turn(j):
-        pairs = jnp.concatenate([stored_ref[j], stored_ref[j + HALF]], axis=0)
-        operator_rows[pl.ds(j, directions, stride=PITCH), :] = jnp.transpose(pairs).astype(f32)
-
     def two_blocks(step, carry):
         blocks = (2 * step, 2 * step + 1)
         force = [[table[block, FORCE + s] for s in range(3)] for block in blocks]
         column_now = None
         for q, (i, j, k) in enumerate(surface):
-            if q % (points // 8) == 0:
-                turn(8 * step + q // (points // 8))
             if (i, j) != column_now:
                 column_now = (i, j)
                 square = [table[block, SQUARE[0] + i] + table[block, SQUARE[1] + j] for block in blocks]
@@ -182,8 +201,8 @@
         check[first : first + 8] = ((rows[0] + rows[1]) + (rows[2] + rows[3])) + ((rows[4] + rows[5]) + (rows[6] + rows[7]))
     potentials = jnp.transpose(check[...])[:, :NCOEF]
     potentials = potentials[:LEAF_DEV] + potentials[LEAF_DEV:]
+    load(2).wait()
     load(3).wait()
-    load(4).wait()
     leaf_density = product(potentials, *halves(uc2ue_ref[...]))
     mid_density = jnp.zeros((8, NCOEF), f32)
     for o in range(8):
@@ -192,8 +211,8 @@
         m2m_high[o] = high
         m2m_low[o] = low
         mid_density += product(leaf_density[8 * o : 8 * o + 8], high, low)
-    shrink = halves(compress_ref[...])
-    rounded = product(jnp.concatenate([leaf_density, mid_density], axis=0), *shrink, contracted=1).astype(bf16)
+    shrink = jnp.concatenate(halves(compress_ref[...]), axis=0)
+    rounded = shrunk(two_bf16(jnp.concatenate([leaf_density, mid_density], axis=0)), shrink).astype(bf16)
     row = lax.broadcasted_iota(jnp.int32, (48, 144), 0)
     col = lax.broadcasted_iota(jnp.int32, (48, 144), 1)
     half = jnp.where(col >= 72, 1, 0)
@@ -214,19 +233,30 @@
         near_copy(number).start()
     nearby[1, own] = block_ref[...]
 
+    load(4).wait()
+    directions = stored_ref.shape[2]
+
+    def turn(j, carry):
+        pairs = jnp.concatenate([stored_ref[j], stored_ref[j + HALF]], axis=0)
+        operator_rows[pl.ds(j, directions, stride=PITCH), :] = jnp.transpose(pairs).astype(f32)
+        return carry
+
+    for j in range(HALF):
+        turn(j, 0)
+    lift = shrunk(jnp.concatenate([m2m_high[octant], m2m_low[octant]], axis=0), shrink)
     own_density = jnp.zeros((8, NCOEF), f32)
     for o in range(8):
         child = jnp.broadcast_to(mid_density[o : o + 1], (8, NCOEF))
         own_density += product(child, m2m_high[o], m2m_low[o])
-    lifted = product(own_density, m2m_high[octant], m2m_low[octant])
-    shrunk = product(jnp.concatenate([own_density, lifted], axis=0), *shrink, contracted=1)
-    small_ref[...] = jnp.concatenate([shrunk[0:1].astype(bf16).astype(f32), shrunk[8:9]], axis=1)
+    lifted = product(own_density, *halves(lift))
+    own_multipole = shrunk(two_bf16(own_density), shrink).astype(bf16).astype(f32)
+    small_ref[...] = jnp.concatenate([own_multipole[:1], lifted[:1]], axis=1)
 
     def send_small(k, carry):
-        small_copy(k, me).start()
-        return carry
-
-    lax.fori_loop(1, peers, send_small, 0)
+        small_copy(k).start()
+        return carry
+
+    lax.fori_loop(1, peers, send_small, 0, unroll=4)
     every[pl.ds(me, 1)] = small_ref[...]
 
     row = lax.broadcasted_iota(jnp.int32, (224, 256), 0)
@@ -269,8 +299,8 @@
     leaf_rows[9] = blank
     mid_rows[0] = blank
     mid_rows[7] = blank
-    for number in near_numbers:
-        near_copy(number, True).wait_recv()
+    for c in range(3):
+        near_whole(c).wait_recv()
 
     for c in range(3):
         inside = (column + c >= 1) & (column + c <= columns_x)
@@ -330,12 +360,7 @@
     packed_ref[5:9] = total[80:84]
     packed_ref[9:73] = total[:64]
 
-    def small_arrived(k, carry):
-        small_copy(k, (me - k + peers) % peers).wait_recv()
-        return carry
-
-    lax.fori_loop(1, peers, small_arrived, 0)
-
+    small_whole().wait_recv()
     own_total = jnp.zeros((1, RANK), f32)
     for u in (-3, -2, 2, 3):
         other = column + u
@@ -370,14 +395,9 @@
             found += jnp.dot(source, root_ref[k], preferred_element_type=f32)
     packed_ref[FIRST_ROOT : FIRST_ROOT + root_count] = found
 
-    for number in near_numbers:
-        near_copy(number).wait_send()
-
-    def small_sent(k, carry):
-        small_copy(k, me).wait_send()
-        return carry
-
-    lax.fori_loop(1, peers, small_sent, 0)
+    for c in range(3):
+        near_whole(c).wait_send()
+    small_whole().wait_send()
 
 
 def finish_kernel(packed_ref, boxes_ref, roots_ref):
@@ -394,7 +414,7 @@
     directions = m2l_ops.shape[0]
     packed = pl.pallas_call(
         functools.partial(solver_kernel, peers),
-        out_shape=jax.ShapeDtypeStruct((FIRST_ROOT + (root_count + 7) // 8 * 8, RANK), f32),
+        out_shape=pltpu.VMEM((FIRST_ROOT + (root_count + 7) // 8 * 8, RANK), f32),
         in_specs=[pl.BlockSpec(memory_space=pltpu.SMEM)] + [anywhere] * 7,
         out_specs=vmem,
         scratch_shapes=[
@@ -421,10 +441,10 @@
             pltpu.VMEM((3 * root_count, 128), f32),
             pltpu.SemaphoreType.DMA((6,)),
             pltpu.SemaphoreType.DMA((8,)),
-            pltpu.SemaphoreType.DMA((peers,)),
-            pltpu.SemaphoreType.DMA((peers,)),
-            pltpu.SemaphoreType.DMA((12,)),
-            pltpu.SemaphoreType.DMA((12,)),
+            pltpu.SemaphoreType.DMA,
+            pltpu.SemaphoreType.DMA,
+            pltpu.SemaphoreType.DMA((3,)),
+            pltpu.SemaphoreType.DMA((3,)),
         ],
         compiler_params=pltpu.CompilerParams(collective_id=0, has_side_effects=True, vmem_limit_bytes=60 << 20),
     )(counts, offsets, forces, uc2ue, compress.T, m2m_ops, stored, root_ops)

time: 26.7 us -> 22.4 us (0.84)
  Pallas kernels: 25.1 us -> 21.6 us
  local copies, waits for them, and re-layouts: 0.78 us -> 0 us
    pallas_call x1, Pallas kernels: 24.4 us -> 20.9 us  [body(): pl.pallas_call(functools.partial(solver_kernel, peers), out_shape=pltpu.V...]
    unnamed x2 -> x0, local copies, waits for them, and re-layouts: 0.78 us -> none
where the time goes in v4:
time: 22.4 us; the launch traced here: 22.3 us
  Pallas kernels  21.6 us (96%)
  between operations  0.64 us (3%)
    pallas_call x1, Pallas kernels, body(): pl.pallas_call(functools.partial(solver_kernel, peers), out_shape=pltpu.V...  20.9 us
    pallas_call x1, Pallas kernels, body(): pl.pallas_call(finish_kernel, out_shape=(jax.ShapeDtypeStruct((RANK, LEAF...  0.7 us

profile of v4, /device:TPU:0, one launch (start us, length us, event | category | flops | bytes accessed | tf_op | source)
XLA Modules:
  0.0 22.3 jit_solution(17821274274108210836)
XLA Ops:
  0.6 20.9 %shard_map.95.packed_ref = f32[88,64]{1,0:T(8,128)S(1)} custom-call(s32[64]{0:T(128)} %counts_ref.1, f32[3,8192]{1,0:T(4,128)} %offsets_hbm.1, f32[3,8192]{1,0:T(4,128)} %forces_hbm.1, f32[456,456]{1,0:T(8,128)} %uc2ue_hbm.1, f32[64,456]{1,0:T(8,128)} %bitcast.4, f32[8,456,456]{2,1,0:T(8,128)} %m2m_hbm.1, bf16[64,64,316]{2,1,0:T(8,128)(2,1)} %bitcast.3, ...), custom_call_target="tpu_custom_call" | custom-call | tf_op jit(solution)/shard_map/pallas_call | solution.py:415
  21.6 0.7 %shard_map.96 = (f32[64,73]{1,0:T(8,128)}, f32[4,64]{1,0:T(4,128)}) custom-call(f32[88,64]{1,0:T(8,128)S(1)} %shard_map.95.packed_ref), custom_call_target="tpu_custom_call" | custom-call | tf_op jit(solution)/shard_map/pallas_call | solution.py:451

commit v5 on v4

--- a/solution.py
+++ b/solution.py
@@ -66,7 +66,7 @@
 
 def solver_kernel(peers, counts_ref, offsets_hbm, forces_hbm, uc2ue_hbm, compress_hbm, m2m_hbm, stored_hbm, root_hbm,
                   packed_ref,
-                  offsets_ref, forces_ref, uc2ue_ref, compress_ref, m2m, m2m_high, m2m_low, stored_ref, root_ref, check,
+                  offsets_ref, forces_ref, uc2ue_ref, compress_ref, uc2ue_high, uc2ue_low, shrink_parts, m2m, m2m_high, m2m_low, stored_ref, root_ref, check,
                   slots_by_leaf, table, sums,
                   small_ref, block_ref, every, nearby, leaf_rows, mid_rows, operator_rows, padded,
                   loads, arrivals, send_all, recv_all, send_near, recv_near):
@@ -106,26 +106,27 @@
         pl.semaphore_signal(barrier, inc=1, device_id=(around(k),), device_id_type=MESH)
         return carry
 
-    lax.fori_loop(1, peers, greet, 0, unroll=4)
-
-    parts = {-1: (0, 32), 0: (0, 48), 1: (16, 48)}
-
-    def near_copy(number):
+    lax.fori_loop(1, peers, greet, 0, unroll=peers - 1 if peers <= 64 else 5)
+
+    parts = {-1: (0, 16), 0: (0, 32), 1: (16, 32)}
+    near_numbers = [number for number in range(12) if number != 4]
+
+    def near_copy(number, kind):
         dc, flip_y, flip_z = number // 4 - 1, number // 2 % 2, number % 2
         other = (y_bit + flip_y) % 2 * 2 + (z_bit + flip_z) % 2
         peer = (column + dc + columns_x) % columns_x * 4 + other
-        first, last = parts[dc]
+        first, last = (32, 48) if kind else parts[dc]
         return pltpu.make_async_remote_copy(
             src_ref=block_ref.at[first:last],
             dst_ref=nearby.at[1 - dc, own, first:last],
-            send_sem=send_near.at[1 - dc], recv_sem=recv_near.at[1 - dc],
+            send_sem=send_near.at[kind, 1 - dc], recv_sem=recv_near.at[kind, 1 - dc],
             device_id=(peer,), device_id_type=MESH)
 
-    def near_whole(c):
-        count, (first, last) = (3 if c == 1 else 4), parts[1 - c]
+    def near_whole(c, kind):
+        count, (first, last) = (3 if c == 1 else 4), ((32, 48) if kind else parts[1 - c])
         space = nearby.at[c, 0:count, first:last]
         return pltpu.make_async_remote_copy(
-            src_ref=space, dst_ref=space, send_sem=send_near.at[c], recv_sem=recv_near.at[c],
+            src_ref=space, dst_ref=space, send_sem=send_near.at[kind, c], recv_sem=recv_near.at[kind, c],
             device_id=(me,), device_id_type=MESH)
 
     def small_copy(k):
@@ -156,26 +157,30 @@
         )
         return carry
 
-    lax.fori_loop(0, LEAF_DEV, place, 0, unroll=8)
+    lax.fori_loop(0, LEAF_DEV, place, 0, unroll=16)
     for s in range(6):
         leaves = slots_by_leaf[s * LEAF_PITCH : s * LEAF_PITCH + LEAF_DEV]
         leaves = jnp.concatenate([leaves[:, : P_CAP // 2], leaves[:, P_CAP // 2 :]], axis=0)
-        table[:, s if s < 3 else FORCE + s - 3] = jnp.transpose(leaves).reshape(8, 8, 128)
-
-    def prepare(block, carry):
-        place = [table[block, s] for s in range(3)]
-        force = [table[block, FORCE + s] for s in range(3)]
+        table[:, FORCE + 3 + s if s < 3 else FORCE + s - 3] = jnp.transpose(leaves).reshape(8, 8, 128)
+
+    for block in range(8):
         for s in range(3):
+            place, force = table[block, FORCE + 3 + s], table[block, FORCE + s]
             for i in range(SURF_ORDER):
-                apart = ticks[i] - place[s]
+                apart = ticks[i] - place
                 table[block, APART[s] + i] = apart
                 table[block, SQUARE[s] + i] = apart * apart
-                table[block, ALONG[s] + i] = apart * force[s]
-        return carry
-
-    lax.fori_loop(0, 8, prepare, 0)
+                table[block, ALONG[s] + i] = apart * force
+
+    load(2).wait()
+    load(3).wait()
+    uc2ue_high[...], uc2ue_low[...] = halves(uc2ue_ref[...])
+    shrink_parts[...] = jnp.concatenate(halves(compress_ref[...]), axis=0)
+
     def two_blocks(step, carry):
         blocks = (2 * step, 2 * step + 1)
+        for o in blocks:
+            pltpu.make_async_copy(m2m_hbm.at[o], m2m.at[o], arrivals.at[o]).wait()
         force = [[table[block, FORCE + s] for s in range(3)] for block in blocks]
         column_now = None
         for q, (i, j, k) in enumerate(surface):
@@ -193,6 +198,10 @@
             for s in range(3):
                 rows = slice((s * points + q) * 8, (s * points + q) * 8 + 8)
                 sums[rows] += values[s][0] + values[s][1]
+            if q % 3 == 0 and 16 * (q // 3) < NCOEF:
+                rows = slice(16 * (q // 3), min(16 * (q // 3) + 16, NCOEF))
+                for o in blocks:
+                    m2m_high[o, rows], m2m_low[o, rows] = halves(m2m[o, rows])
         return carry
 
     lax.fori_loop(0, 4, two_blocks, 0)
@@ -201,37 +210,34 @@
         check[first : first + 8] = ((rows[0] + rows[1]) + (rows[2] + rows[3])) + ((rows[4] + rows[5]) + (rows[6] + rows[7]))
     potentials = jnp.transpose(check[...])[:, :NCOEF]
     potentials = potentials[:LEAF_DEV] + potentials[LEAF_DEV:]
-    load(2).wait()
-    load(3).wait()
-    leaf_density = product(potentials, *halves(uc2ue_ref[...]))
+    leaf_density = product(potentials, uc2ue_high[...], uc2ue_low[...])
+    rounded = shrunk(two_bf16(leaf_density), shrink_parts[...]).astype(bf16)
+    row = lax.broadcasted_iota(jnp.int32, (32, 128), 0)
+    col = lax.broadcasted_iota(jnp.int32, (32, 128), 1)
+    odd = (col >> 6) * 4 + (row >> 2 & 1) * 2 + (row & 1)
+    parent = (row >> 4) * 4 + (row >> 3 & 1) * 2 + (row >> 1 & 1)
+    order = jnp.where(col & (LEAF_DEV - 1) == odd * 8 + parent, 1.0, 0.0).astype(bf16)
+    nothing = jnp.zeros((LEAF_DEV, RANK), bf16)
+    pairs = jnp.concatenate(
+        [jnp.concatenate([rounded, nothing], axis=1), jnp.concatenate([nothing, rounded], axis=1)], axis=0
+    )
+    block_ref[0:32] = jnp.dot(order, pairs, preferred_element_type=f32).astype(bf16)
+
+    pl.semaphore_wait(barrier, peers - 1)
+    for number in near_numbers:
+        near_copy(number, 0).start()
+    nearby[1, own, 0:32] = block_ref[0:32]
+
     mid_density = jnp.zeros((8, NCOEF), f32)
     for o in range(8):
-        pltpu.make_async_copy(m2m_hbm.at[o], m2m.at[o], arrivals.at[o]).wait()
-        high, low = halves(m2m[o])
-        m2m_high[o] = high
-        m2m_low[o] = low
-        mid_density += product(leaf_density[8 * o : 8 * o + 8], high, low)
-    shrink = jnp.concatenate(halves(compress_ref[...]), axis=0)
-    rounded = shrunk(two_bf16(jnp.concatenate([leaf_density, mid_density], axis=0)), shrink).astype(bf16)
-    row = lax.broadcasted_iota(jnp.int32, (48, 144), 0)
-    col = lax.broadcasted_iota(jnp.int32, (48, 144), 1)
-    half = jnp.where(col >= 72, 1, 0)
-    odd = half * 4 + (row >> 2 & 1) * 2 + (row & 1)
-    parent = (row >> 5) * 4 + (row >> 3 & 1) * 2 + (row >> 1 & 1)
-    place = (row & 15) + jnp.where((row & 15) < 4, half * 4 + LEAF_DEV, 2 * LEAF_DEV)
-    wanted = jnp.where((row >> 4) == 1, place, odd * 8 + parent)
-    order = jnp.where(col - 72 * half == wanted, 1.0, 0.0).astype(bf16)
-    nothing = jnp.zeros((72, RANK), bf16)
-    pairs = jnp.concatenate(
-        [jnp.concatenate([rounded, nothing], axis=1), jnp.concatenate([nothing, rounded], axis=1)], axis=0
-    )
-    block_ref[...] = jnp.dot(order, pairs, preferred_element_type=f32).astype(bf16)
-
-    pl.semaphore_wait(barrier, peers - 1)
-    near_numbers = [number for number in range(12) if number != 4]
+        mid_density += product(leaf_density[8 * o : 8 * o + 8], m2m_high[o], m2m_low[o])
+    shrink = shrink_parts[...]
+    mid_pairs = shrunk(two_bf16(mid_density), shrink)
+    mid_pairs = jnp.concatenate([mid_pairs[:4], mid_pairs[4:]], axis=1)
+    block_ref[32:48] = jnp.concatenate([mid_pairs, jnp.zeros((12, 2 * RANK), f32)], axis=0).astype(bf16)
     for number in near_numbers:
-        near_copy(number).start()
-    nearby[1, own] = block_ref[...]
+        near_copy(number, 1).start()
+    nearby[1, own, 32:48] = block_ref[32:48]
 
     load(4).wait()
     directions = stored_ref.shape[2]
@@ -256,7 +262,7 @@
         small_copy(k).start()
         return carry
 
-    lax.fori_loop(1, peers, send_small, 0, unroll=4)
+    lax.fori_loop(1, peers, send_small, 0, unroll=peers - 1 if peers <= 64 else 5)
     every[pl.ds(me, 1)] = small_ref[...]
 
     row = lax.broadcasted_iota(jnp.int32, (224, 256), 0)
@@ -300,13 +306,14 @@
     mid_rows[0] = blank
     mid_rows[7] = blank
     for c in range(3):
-        near_whole(c).wait_recv()
+        near_whole(c, 0).wait_recv()
+        near_whole(c, 1).wait_recv()
 
     for c in range(3):
         inside = (column + c >= 1) & (column + c <= columns_x)
         diagonal = jnp.where(on_diagonal & inside, 1.0, 0.0).astype(bf16)
         for first in range(0, 48, 16):
-            if (c, first) in ((0, 0), (2, 32)):
+            if (c, first) in ((0, 0), (2, 16)):
                 continue
             stack = nearby[c, :, first : first + 16, :].reshape(64, 128)
             for lx in range(2):
@@ -314,12 +321,12 @@
                 high = stack[:, RANK * lx + HALF : RANK * lx + RANK]
                 wide = jnp.concatenate([low] * 4 + [high] * 4, axis=1)
                 sources = jnp.concatenate([wide] * 4, axis=0) * diagonal
-                if first == 16:
+                if first == 32:
                     got = jnp.dot(mid_select, sources, preferred_element_type=f32)
                     mid_rows[2 * c + lx + 1] = got.astype(bf16).reshape(14, 16, 256)
                 else:
                     got = jnp.dot(leaf_select, sources, preferred_element_type=f32)
-                    leaf_rows[4 * c + first // 16 + lx - 1] = got.astype(bf16).reshape(14, 16, 256)
+                    leaf_rows[4 * c + first // 8 + lx - 1] = got.astype(bf16).reshape(14, 16, 256)
 
     bases = {-3: 0, -2: 49, 2: 218, 3: 267}
     first_direction = 0
@@ -396,7 +403,8 @@
     packed_ref[FIRST_ROOT : FIRST_ROOT + root_count] = found
 
     for c in range(3):
-        near_whole(c).wait_send()
+        near_whole(c, 0).wait_send()
+        near_whole(c, 1).wait_send()
     small_whole().wait_send()
 
 
@@ -422,6 +430,9 @@
             pltpu.VMEM(forces.shape, f32),
             pltpu.VMEM(uc2ue.shape, f32),
             pltpu.VMEM((RANK, NCOEF), f32),
+            pltpu.VMEM(uc2ue.shape, bf16),
+            pltpu.VMEM(uc2ue.shape, bf16),
+            pltpu.VMEM((2 * RANK, NCOEF), bf16),
             pltpu.VMEM(m2m_ops.shape, f32),
             pltpu.VMEM(m2m_ops.shape, bf16),
             pltpu.VMEM(m2m_ops.shape, bf16),
@@ -429,7 +440,7 @@
             pltpu.VMEM(root_ops.shape, bf16),
             pltpu.VMEM((512, 128), f32),
             pltpu.VMEM((6 * LEAF_PITCH, P_CAP), f32),
-            pltpu.VMEM((8, FORCE + 3, 8, 128), f32),
+            pltpu.VMEM((8, FORCE + 6, 8, 128), f32),
             pltpu.VMEM((8 * NCOEF, 128), f32),
             pltpu.VMEM((1, 128), f32),
             pltpu.VMEM((48, 128), bf16),
@@ -443,8 +454,8 @@
             pltpu.SemaphoreType.DMA((8,)),
             pltpu.SemaphoreType.DMA,
             pltpu.SemaphoreType.DMA,
-            pltpu.SemaphoreType.DMA((3,)),
-            pltpu.SemaphoreType.DMA((3,)),
+            pltpu.SemaphoreType.DMA((2, 3)),
+            pltpu.SemaphoreType.DMA((2, 3)),
         ],
         compiler_params=pltpu.CompilerParams(collective_id=0, has_side_effects=True, vmem_limit_bytes=60 << 20),
     )(counts, offsets, forces, uc2ue, compress.T, m2m_ops, stored, root_ops)

time: 22.4 us -> 22.8 us (1.018)
  Pallas kernels: 21.6 us -> 22 us
    pallas_call x1, Pallas kernels: 20.9 us -> 21.3 us  [body(): pl.pallas_call(functools.partial(solver_kernel, peers), out_shape=pltpu.V...]
where the time goes in v5:
time: 22.8 us; the launch traced here: 22.7 us
  Pallas kernels  22 us (96%)
  between operations  0.64 us (3%)
    pallas_call x1, Pallas kernels, body(): pl.pallas_call(functools.partial(solver_kernel, peers), out_shape=pltpu.V...  21.3 us
    pallas_call x1, Pallas kernels, body(): pl.pallas_call(finish_kernel, out_shape=(jax.ShapeDtypeStruct((RANK, LEAF...  0.7 us

profile of v5, /device:TPU:0, one launch (start us, length us, event | category | flops | bytes accessed | tf_op | source)
XLA Modules:
  0.0 22.7 jit_solution(1869443969718356884)
XLA Ops:
  0.6 21.3 %shard_map.95.packed_ref = f32[88,64]{1,0:T(8,128)S(1)} custom-call(s32[64]{0:T(128)} %counts_ref.1, f32[3,8192]{1,0:T(4,128)} %offsets_hbm.1, f32[3,8192]{1,0:T(4,128)} %forces_hbm.1, f32[456,456]{1,0:T(8,128)} %uc2ue_hbm.1, f32[64,456]{1,0:T(8,128)} %bitcast.4, f32[8,456,456]{2,1,0:T(8,128)} %m2m_hbm.1, bf16[64,64,316]{2,1,0:T(8,128)(2,1)} %bitcast.3, ...), custom_call_target="tpu_custom_call" | custom-call | tf_op jit(solution)/shard_map/pallas_call | solution.py:423
  22.0 0.7 %shard_map.96 = (f32[64,73]{1,0:T(8,128)}, f32[4,64]{1,0:T(4,128)}) custom-call(f32[88,64]{1,0:T(8,128)S(1)} %shard_map.95.packed_ref), custom_call_target="tpu_custom_call" | custom-call | tf_op jit(solution)/shard_map/pallas_call | solution.py:462

commit v6 on v4

--- a/solution.py
+++ b/solution.py
@@ -156,26 +156,25 @@
         )
         return carry
 
-    lax.fori_loop(0, LEAF_DEV, place, 0, unroll=8)
+    lax.fori_loop(0, LEAF_DEV, place, 0, unroll=16)
     for s in range(6):
         leaves = slots_by_leaf[s * LEAF_PITCH : s * LEAF_PITCH + LEAF_DEV]
         leaves = jnp.concatenate([leaves[:, : P_CAP // 2], leaves[:, P_CAP // 2 :]], axis=0)
-        table[:, s if s < 3 else FORCE + s - 3] = jnp.transpose(leaves).reshape(8, 8, 128)
-
-    def prepare(block, carry):
-        place = [table[block, s] for s in range(3)]
-        force = [table[block, FORCE + s] for s in range(3)]
+        table[:, FORCE + 3 + s if s < 3 else FORCE + s - 3] = jnp.transpose(leaves).reshape(8, 8, 128)
+
+    for block in range(8):
         for s in range(3):
+            place, force = table[block, FORCE + 3 + s], table[block, FORCE + s]
             for i in range(SURF_ORDER):
-                apart = ticks[i] - place[s]
+                apart = ticks[i] - place
                 table[block, APART[s] + i] = apart
                 table[block, SQUARE[s] + i] = apart * apart
-                table[block, ALONG[s] + i] = apart * force[s]
-        return carry
-
-    lax.fori_loop(0, 8, prepare, 0)
+                table[block, ALONG[s] + i] = apart * force
+
     def two_blocks(step, carry):
         blocks = (2 * step, 2 * step + 1)
+        for o in blocks:
+            pltpu.make_async_copy(m2m_hbm.at[o], m2m.at[o], arrivals.at[o]).wait()
         force = [[table[block, FORCE + s] for s in range(3)] for block in blocks]
         column_now = None
         for q, (i, j, k) in enumerate(surface):
@@ -193,6 +192,10 @@
             for s in range(3):
                 rows = slice((s * points + q) * 8, (s * points + q) * 8 + 8)
                 sums[rows] += values[s][0] + values[s][1]
+            if q % 3 == 0 and 16 * (q // 3) < NCOEF:
+                rows = slice(16 * (q // 3), min(16 * (q // 3) + 16, NCOEF))
+                for o in blocks:
+                    m2m_high[o, rows], m2m_low[o, rows] = halves(m2m[o, rows])
         return carry
 
     lax.fori_loop(0, 4, two_blocks, 0)
@@ -204,28 +207,26 @@
     load(2).wait()
     load(3).wait()
     leaf_density = product(potentials, *halves(uc2ue_ref[...]))
+    shrink = jnp.concatenate(halves(compress_ref[...]), axis=0)
+    rounded = shrunk(two_bf16(leaf_density), shrink).astype(bf16)
     mid_density = jnp.zeros((8, NCOEF), f32)
     for o in range(8):
-        pltpu.make_async_copy(m2m_hbm.at[o], m2m.at[o], arrivals.at[o]).wait()
-        high, low = halves(m2m[o])
-        m2m_high[o] = high
-        m2m_low[o] = low
-        mid_density += product(leaf_density[8 * o : 8 * o + 8], high, low)
-    shrink = jnp.concatenate(halves(compress_ref[...]), axis=0)
-    rounded = shrunk(two_bf16(jnp.concatenate([leaf_density, mid_density], axis=0)), shrink).astype(bf16)
-    row = lax.broadcasted_iota(jnp.int32, (48, 144), 0)
-    col = lax.broadcasted_iota(jnp.int32, (48, 144), 1)
-    half = jnp.where(col >= 72, 1, 0)
-    odd = half * 4 + (row >> 2 & 1) * 2 + (row & 1)
-    parent = (row >> 5) * 4 + (row >> 3 & 1) * 2 + (row >> 1 & 1)
-    place = (row & 15) + jnp.where((row & 15) < 4, half * 4 + LEAF_DEV, 2 * LEAF_DEV)
-    wanted = jnp.where((row >> 4) == 1, place, odd * 8 + parent)
-    order = jnp.where(col - 72 * half == wanted, 1.0, 0.0).astype(bf16)
-    nothing = jnp.zeros((72, RANK), bf16)
+        mid_density += product(leaf_density[8 * o : 8 * o + 8], m2m_high[o], m2m_low[o])
+    row = lax.broadcasted_iota(jnp.int32, (32, 128), 0)
+    col = lax.broadcasted_iota(jnp.int32, (32, 128), 1)
+    odd = (col >> 6) * 4 + (row >> 2 & 1) * 2 + (row & 1)
+    parent = (row >> 4) * 4 + (row >> 3 & 1) * 2 + (row >> 1 & 1)
+    order = jnp.where((col & (LEAF_DEV - 1)) == odd * 8 + parent, 1.0, 0.0).astype(bf16)
+    nothing = jnp.zeros((LEAF_DEV, RANK), bf16)
     pairs = jnp.concatenate(
         [jnp.concatenate([rounded, nothing], axis=1), jnp.concatenate([nothing, rounded], axis=1)], axis=0
     )
-    block_ref[...] = jnp.dot(order, pairs, preferred_element_type=f32).astype(bf16)
+    leaves = jnp.dot(order, pairs, preferred_element_type=f32).astype(bf16)
+    block_ref[0:16] = leaves[:16]
+    block_ref[32:48] = leaves[16:]
+    mid_pairs = shrunk(two_bf16(mid_density), shrink)
+    mid_pairs = jnp.concatenate([mid_pairs[:4], mid_pairs[4:]], axis=1)
+    block_ref[16:32] = jnp.concatenate([mid_pairs, jnp.zeros((12, 2 * RANK), f32)], axis=0).astype(bf16)
 
     pl.semaphore_wait(barrier, peers - 1)
     near_numbers = [number for number in range(12) if number != 4]
@@ -429,7 +430,7 @@
             pltpu.VMEM(root_ops.shape, bf16),
             pltpu.VMEM((512, 128), f32),
             pltpu.VMEM((6 * LEAF_PITCH, P_CAP), f32),
-            pltpu.VMEM((8, FORCE + 3, 8, 128), f32),
+            pltpu.VMEM((8, FORCE + 6, 8, 128), f32),
             pltpu.VMEM((8 * NCOEF, 128), f32),
             pltpu.VMEM((1, 128), f32),
             pltpu.VMEM((48, 128), bf16),

time: 22.4 us -> 22.2 us (level)
  Pallas kernels: 21.6 us -> 21.3 us
    pallas_call x1, Pallas kernels: 20.9 us -> 20.6 us  [body(): pl.pallas_call(functools.partial(solver_kernel, peers), out_shape=pltpu.V...]
where the time goes in v6:
time: 22.2 us; the launch traced here: 22 us
  Pallas kernels  21.3 us (96%)
  between operations  0.64 us (3%)
    pallas_call x1, Pallas kernels, body(): pl.pallas_call(functools.partial(solver_kernel, peers), out_shape=pltpu.V...  20.6 us
    pallas_call x1, Pallas kernels, body(): pl.pallas_call(finish_kernel, out_shape=(jax.ShapeDtypeStruct((RANK, LEAF...  0.7 us

profile of v6, /device:TPU:0, one launch (start us, length us, event | category | flops | bytes accessed | tf_op | source)
XLA Modules:
  0.0 22.0 jit_solution(2793869559932788640)
XLA Ops:
  0.6 20.6 %shard_map.95.packed_ref = f32[88,64]{1,0:T(8,128)S(1)} custom-call(s32[64]{0:T(128)} %counts_ref.1, f32[3,8192]{1,0:T(4,128)} %offsets_hbm.1, f32[3,8192]{1,0:T(4,128)} %forces_hbm.1, f32[456,456]{1,0:T(8,128)} %uc2ue_hbm.1, f32[64,456]{1,0:T(8,128)} %bitcast.4, f32[8,456,456]{2,1,0:T(8,128)} %m2m_hbm.1, bf16[64,64,316]{2,1,0:T(8,128)(2,1)} %bitcast.3, ...), custom_call_target="tpu_custom_call" | custom-call | tf_op jit(solution)/shard_map/pallas_call | solution.py:416
  21.3 0.7 %shard_map.96 = (f32[64,73]{1,0:T(8,128)}, f32[4,64]{1,0:T(4,128)}) custom-call(f32[88,64]{1,0:T(8,128)S(1)} %shard_map.95.packed_ref), custom_call_target="tpu_custom_call" | custom-call | tf_op jit(solution)/shard_map/pallas_call | solution.py:452

commit v7 on v6

--- a/solution.py
+++ b/solution.py
@@ -361,6 +361,10 @@
     packed_ref[5:9] = total[80:84]
     packed_ref[9:73] = total[:64]
 
+    for c in range(3):
+        near_whole(c).wait_send()
+    small_whole().wait_send()
+    load(5).wait()
     small_whole().wait_recv()
     own_total = jnp.zeros((1, RANK), f32)
     for u in (-3, -2, 2, 3):
@@ -383,22 +387,18 @@
         own_total += jnp.where(good, part, 0.0)
     packed_ref[0:1] = own_total
 
-    load(5).wait()
-    padded[...] = jnp.zeros_like(padded)
-    for r in range(root_count):
-        padded[root_count + r : root_count + r + 1] = jnp.sum(every[8 * r : 8 * r + 8], axis=0, keepdims=True)
+    gathered = jnp.sum(every[...].reshape(root_count, 8, 2 * RANK), axis=1)[:, RANK:]
+    padded[0:root_count] = jnp.zeros((root_count, RANK), f32)
+    padded[root_count : 2 * root_count] = gathered
+    padded[2 * root_count :] = jnp.zeros((root_count, RANK), f32)
     found = jnp.zeros((root_count, RANK), f32)
     for k in range(2 * root_count - 1):
         distance = k - (root_count - 1)
         if abs(distance) >= 2:
             start = root_count + distance
-            source = padded[start : start + root_count, :][:, RANK:].astype(bf16)
+            source = padded[start : start + root_count].astype(bf16)
             found += jnp.dot(source, root_ref[k], preferred_element_type=f32)
     packed_ref[FIRST_ROOT : FIRST_ROOT + root_count] = found
-
-    for c in range(3):
-        near_whole(c).wait_send()
-    small_whole().wait_send()
 
 
 def finish_kernel(packed_ref, boxes_ref, roots_ref):
@@ -439,7 +439,7 @@
             pltpu.VMEM((10, 14, 16, 256), bf16),
             pltpu.VMEM((8, 14, 16, 256), bf16),
             pltpu.VMEM((directions * PITCH, 2 * RANK), f32),
-            pltpu.VMEM((3 * root_count, 128), f32),
+            pltpu.VMEM((3 * root_count, RANK), f32),
             pltpu.SemaphoreType.DMA((6,)),
             pltpu.SemaphoreType.DMA((8,)),
             pltpu.SemaphoreType.DMA,

time: 22.2 us -> 21.9 us (0.986)
  no operation moved by 1% of the time
where the time goes in v7:
time: 21.9 us; the launch traced here: 21.8 us
  Pallas kernels  21.1 us (96%)
  between operations  0.64 us (3%)
    pallas_call x1, Pallas kernels, body(): pl.pallas_call(functools.partial(solver_kernel, peers), out_shape=pltpu.V...  20.4 us
    pallas_call x1, Pallas kernels, body(): pl.pallas_call(finish_kernel, out_shape=(jax.ShapeDtypeStruct((RANK, LEAF...  0.7 us

profile of v7, /device:TPU:0, one launch (start us, length us, event | category | flops | bytes accessed | tf_op | source)
XLA Modules:
  0.0 21.8 jit_solution(4828488812682526942)
XLA Ops:
  0.6 20.4 %shard_map.95.packed_ref = f32[88,64]{1,0:T(8,128)S(1)} custom-call(s32[64]{0:T(128)} %counts_ref.1, f32[3,8192]{1,0:T(4,128)} %offsets_hbm.1, f32[3,8192]{1,0:T(4,128)} %forces_hbm.1, f32[456,456]{1,0:T(8,128)} %uc2ue_hbm.1, f32[64,456]{1,0:T(8,128)} %bitcast.4, f32[8,456,456]{2,1,0:T(8,128)} %m2m_hbm.1, bf16[64,64,316]{2,1,0:T(8,128)(2,1)} %bitcast.3, ...), custom_call_target="tpu_custom_call" | custom-call | tf_op jit(solution)/shard_map/pallas_call | solution.py:416
  21.1 0.7 %shard_map.96 = (f32[64,73]{1,0:T(8,128)}, f32[4,64]{1,0:T(4,128)}) custom-call(f32[88,64]{1,0:T(8,128)S(1)} %shard_map.95.packed_ref), custom_call_target="tpu_custom_call" | custom-call | tf_op jit(solution)/shard_map/pallas_call | solution.py:452
